TPU v7x, 32 devices: a whole 2x2x4 slice. The times are simulated.
32 devices in a mesh: dp: 4 (over z), seq: 4 (over x, core), mp: 2 (over y).
Axes of the slice: x: 2, y: 2, z: 4, core: 2. Of those that a mesh axis runs over, the one named last changes fastest.
Arguments:
- queries: bfloat16 [2048, 4096], P(('dp', 'seq'), 'mp'), may hold values from -2 to 2
- key_rows: bfloat16 [2048, 4096], P(('dp', 'seq'), 'mp'), may hold values from -2 to 2
- value_rows: bfloat16 [2048, 4096], P(('dp', 'seq'), 'mp'), may hold values from -6 to 6
- row_plan: int32 [4, 4], replicated, may hold values from 0 to 40, as said below
- segments: int32 [4, 512], P('dp', 'seq'), may hold values from 0 to 5, never falling along the last dimension, each value on 1 to 256 neighbouring positions
- norm_gain: float32 [4096], P('mp'), may hold values from 0.5 to 1.5
- out_weight: bfloat16 [4096, 3072], P('mp'), may hold values from -0.09375 to 0.09375
- out_grad: bfloat16 [2048, 3072], P(('dp', 'seq'), 'mp'), may hold values from -6 to 6
Outputs:
- normed: bfloat16 [2048, 4096], P(('dp', 'seq'), 'mp')
- query_grad: bfloat16 [2048, 4096], P(('dp', 'seq'), 'mp')
- key_grad: bfloat16 [2048, 4096], P(('dp', 'seq'), 'mp')
- value_grad: bfloat16 [2048, 4096], P(('dp', 'seq'), 'mp')
- weight_grad: float32 [3072, 4096], P(('dp', 'seq'), 'mp')
Inputs may be any that keep to these rules, and one draw needn't show every extreme that they name: Each row and each column of row_plan sums to 128; the plan holds for every sequence shard alike; an arriving group's rows for group 0 come first, then those for group 1, and so on. `segments`: documents never cross data groups.
All inputs are finite; a program needn't handle non-finite values.
Results may differ from a plain program's by a relative error of at most 0.0064.
Values may be sent and summed in bfloat16 or wider, within the bound.
A program may use at most 128 MiB of HBM per device.

v0:
```python
import jax
import jax.numpy as jnp
from jax import lax
from jax.sharding import PartitionSpec as P

HS = 128


NORM_EPS = 1e-06
HIGH = lax.Precision.HIGHEST


def prefix(x, axis, combine, identity, reverse):
    peers, place = (lax.axis_size(axis), lax.axis_index(axis))
    everything = jax.tree.map(lambda part: lax.all_gather(part, axis), x)
    start = jax.tree.map(
        lambda part, zero: jnp.broadcast_to(jnp.asarray(zero, part.dtype), part.shape), x, identity
    )

    def lap(k, before):
        at = peers - 1 - k if reverse else k
        reached = at > place if reverse else at < place
        new = combine(before, jax.tree.map(lambda part: part[at], everything))
        return jax.tree.map(lambda a, b: jnp.where(reached, a, b), new, before)

    return lax.fori_loop(0, peers, lap, start)


def rms_scale(attn, gain_heads):
    power = jnp.mean(attn * attn, axis=-1, keepdims=True)
    return attn * lax.rsqrt(power + NORM_EPS) * gain_heads


def link_states(earlier, later):
    early_state, early_id = earlier
    late_state, late_id = later
    absent = late_id[0] < 0.0
    joined = early_id[0] == late_id[0]
    merged = late_state + jnp.where(joined, early_state, jnp.zeros_like(early_state))
    return (jnp.where(absent, early_state, merged), jnp.where(absent, early_id, late_id))


def local(queries, key_rows, value_rows, row_plan, segments, norm_gain, out_weight, out_grad):
    row_total = queries.shape[0]
    width = queries.shape[1]
    heads = width // HS
    groups = lax.axis_size("dp")
    my_group = lax.axis_index("dp")
    capacity = row_total // min(groups, 8) + row_total // 16
    send_start = jnp.cumsum(row_plan, axis=1) - row_plan
    recv_start = jnp.cumsum(row_plan, axis=0) - row_plan
    slots = jnp.arange(capacity, dtype=jnp.int32)
    my_send = jnp.take(send_start, my_group, axis=0)
    send_index = jnp.minimum(my_send[:, None] + slots[None, :], row_total - 1).reshape(-1)
    packed = (
        jnp.take(queries, send_index, axis=0),
        jnp.take(key_rows, send_index, axis=0),
        jnp.take(value_rows, send_index, axis=0),
    )
    arrived = (
        lax.all_to_all(packed[0], "dp", split_axis=0, concat_axis=0, tiled=True),
        lax.all_to_all(packed[1], "dp", split_axis=0, concat_axis=0, tiled=True),
        lax.all_to_all(packed[2], "dp", split_axis=0, concat_axis=0, tiled=True),
    )
    positions = jnp.arange(row_total, dtype=jnp.int32)
    my_start = jnp.take(recv_start, my_group, axis=1)
    my_end = my_start + jnp.take(row_plan, my_group, axis=1)
    source = jnp.sum((my_end[None, :] <= positions[:, None]).astype(jnp.int32), axis=1)
    pick = source * capacity + positions - jnp.take(my_start, source)
    q_half = jnp.take(arrived[0], pick, axis=0).reshape(row_total, heads, HS)
    k_half = jnp.take(arrived[1], pick, axis=0).reshape(row_total, heads, HS)
    v_half = jnp.take(arrived[2], pick, axis=0).reshape(row_total, heads, HS)
    query = q_half.astype(jnp.float32)
    keyv = k_half.astype(jnp.float32)
    value = v_half.astype(jnp.float32)
    seg_ids = segments[0]
    seg_f = seg_ids.astype(jnp.float32)
    causal = positions[None, :] <= positions[:, None]
    same_doc = (causal & (seg_ids[:, None] == seg_ids[None, :])).astype(jnp.float32)
    scores = (
        jnp.einsum("thd,shd->hts", q_half, k_half, preferred_element_type=jnp.float32)
        * same_doc[None]
    )
    scores_half = scores.astype(jnp.bfloat16)
    inner = jnp.einsum("hts,she->the", scores_half, v_half, preferred_element_type=jnp.float32)
    tail = seg_f == seg_f[-1]
    k_tail = jnp.where(tail[:, None, None], k_half, jnp.zeros_like(k_half))
    local_state = jnp.einsum("thd,the->hde", k_tail, v_half, preferred_element_type=jnp.float32)
    identity = (jnp.zeros_like(local_state), jnp.full((1,), -1.0, jnp.float32))
    state_in, id_in = prefix((local_state, seg_f[-1:]), "seq", link_states, identity, False)
    carried = (seg_f == id_in[0]).astype(jnp.float32)
    attn = (
        inner + jnp.einsum("thd,hde->the", query, state_in, precision=HIGH) * carried[:, None, None]
    )
    gain_heads = norm_gain.reshape(heads, HS)
    normed_f, pull = jax.vjp(lambda a: rms_scale(a, gain_heads), attn)
    normed = normed_f.reshape(row_total, width).astype(jnp.bfloat16)
    full_grad = lax.all_gather(out_grad, "mp", axis=1, tiled=True)
    d_normed = lax.dot_general(
        full_grad, out_weight, (((1,), (1,)), ((), ())), preferred_element_type=jnp.float32
    )
    d_attn = pull(d_normed.reshape(row_total, heads, HS))[0]
    d_half = d_attn.astype(jnp.bfloat16)
    dprob = (
        jnp.einsum("the,she->hts", d_half, v_half, preferred_element_type=jnp.float32)
        * same_doc[None]
    )
    dprob_half = dprob.astype(jnp.bfloat16)
    dquery = jnp.einsum("hts,shd->thd", dprob_half, k_half, preferred_element_type=jnp.float32)
    dquery = (
        dquery
        + jnp.einsum("the,hde->thd", d_attn, state_in, precision=HIGH) * carried[:, None, None]
    )
    head_part = (seg_f == seg_f[0]).astype(jnp.float32)
    local_r = jnp.einsum("thd,the->hde", query * head_part[:, None, None], d_attn, precision=HIGH)
    rstate_in, rid_in = prefix((local_r, seg_f[:1]), "seq", link_states, identity, True)
    rev_use = (seg_f == rid_in[0]).astype(jnp.float32)
    dkey = jnp.einsum("hts,thd->shd", dprob_half, q_half, preferred_element_type=jnp.float32)
    dkey = (
        dkey + jnp.einsum("the,hde->thd", value, rstate_in, precision=HIGH) * rev_use[:, None, None]
    )
    dvalue = jnp.einsum("hts,the->she", scores_half, d_half, preferred_element_type=jnp.float32)
    dvalue = (
        dvalue
        + jnp.einsum("thd,hde->the", keyv, rstate_in, precision=HIGH) * rev_use[:, None, None]
    )
    weight_grad = lax.psum_scatter(
        lax.dot_general(
            full_grad, normed, (((0,), (0,)), ((), ())), preferred_element_type=jnp.float32
        ),
        ("dp", "seq"),
        scatter_dimension=0,
        tiled=True,
    )
    return (
        normed,
        dquery.reshape(row_total, width).astype(jnp.bfloat16),
        dkey.reshape(row_total, width).astype(jnp.bfloat16),
        dvalue.reshape(row_total, width).astype(jnp.bfloat16),
        weight_grad,
    )


def solution(mesh):
    placed = (
        P(("dp", "seq"), "mp"),
        P(("dp", "seq"), "mp"),
        P(("dp", "seq"), "mp"),
        P(),
        P("dp", "seq"),
        P("mp"),
        P("mp", None),
        P(("dp", "seq"), "mp"),
    )
    return jax.shard_map(
        local,
        mesh=mesh,
        in_specs=placed,
        out_specs=(
            P(("dp", "seq"), "mp"),
            P(("dp", "seq"), "mp"),
            P(("dp", "seq"), "mp"),
            P(("dp", "seq"), "mp"),
            P(("dp", "seq"), "mp"),
        ),
        check_vma=False,
    )
```

profile of v0, /device:TPU:12, one launch (start us, length us, event | category | flops | bytes accessed | tf_op | source)
XLA Modules:
  0.0 427.4 jit_solution(9844870783483059516)
XLA Ops:
  9.8 1.0 gather_fusion.4
  10.8 2.8 gather_fusion.2
  13.6 1.0 gather_fusion
  14.7 1.3 broadcast_select_fusion.2
  16.0 20.6 %all_to_all.36 = bf16[4,40,2048]{2,1,0:T(8,128)(2,1)S(1)} all-to-all(bf16[4,40,2048]{2,1,0:T(8,128)(2,1)S(1)} %bitcast.157), channel_id=1, replica_groups=mesh['dp'=4,'seq'=4,'mp'=2] {'dp'}, dimensions={0} | all-to-all | bytes 1310720 | tf_op jit(solution)/shard_map/all_to_all | solution.py:61
  36.6 5.4 %all-to-all-start = ((bf16[4,40,2048]{2,1,0:T(8,128)(2,1)}), bf16[4,40,2048]{2,1,0:T(8,128)(2,1)S(1)}, u32[]{:S(2)}, u32[]{:S(2)}) async-start(bf16[4,40,2048]{2,1,0:T(8,128)(2,1)} %bitcast.156), calls=%async_computation | async-start | bytes 1310720 | tf_op jit(solution)/shard_map/all_to_all | solution.py:63
  42.9 12.3 %all-to-all-done = bf16[4,40,2048]{2,1,0:T(8,128)(2,1)S(1)} async-done(((bf16[4,40,2048]{2,1,0:T(8,128)(2,1)}), bf16[4,40,2048]{2,1,0:T(8,128)(2,1)S(1)}, u32[]{:S(2)}, u32[]{:S(2)}) %all-to-all-start) | async-done | bytes 655392 | tf_op jit(solution)/shard_map/all_to_all | solution.py:63
  55.2 6.7 %all-to-all-start.2 = ((bf16[4,40,2048]{2,1,0:T(8,128)(2,1)}), bf16[4,40,2048]{2,1,0:T(8,128)(2,1)S(1)}, u32[]{:S(2)}, u32[]{:S(2)}) async-start(bf16[4,40,2048]{2,1,0:T(8,128)(2,1)} %bitcast.155), calls=%async_computation.2 | async-start | bytes 1310720 | tf_op jit(solution)/shard_map/all_to_all | solution.py:62
  62.5 2.6 compare_and_fusion
  65.2 1.2 fusion.44
  66.4 1.3 compare_convert_fusion.1
  69.6 5.9 %all-to-all-done.2 = bf16[4,40,2048]{2,1,0:T(8,128)(2,1)S(1)} async-done(((bf16[4,40,2048]{2,1,0:T(8,128)(2,1)}), bf16[4,40,2048]{2,1,0:T(8,128)(2,1)S(1)}, u32[]{:S(2)}, u32[]{:S(2)}) %all-to-all-start.2) | async-done | bytes 655392 | tf_op jit(solution)/shard_map/all_to_all | solution.py:62
  76.4 1.2 fusion.35
  78.2 1.3 fusion.19
  80.4 5.6 %all-reduce.2 = (f32[4]{0:T(128)S(1)}, f32[4]{0:T(128)S(1)}) all-reduce(f32[4]{0:T(128)S(1)} %get-tuple-element.397, f32[4]{0:T(128)S(1)} %slice_dynamic-update-slice_fusion), channel_id=2, replica_groups=mesh['dp'=4,'seq'=4,'mp'=2] {'seq'}, use_global_device_ids=true, to_apply=%add | all-reduce | flops 8 | bytes 64
  86.0 11.7 %all_gather.31 = bf16[128,3072]{1,0:T(8,128)(2,1)S(1)} all-gather(bf16[128,1536]{1,0:T(8,128)(2,1)S(1)} %copy-done.13), channel_id=1, replica_groups=mesh['dp'=4,'seq'=4,'mp'=2] {'mp'}, dimensions={1}, use_global_device_ids=true | all-gather | bytes 1179648 | tf_op jit(solution)/shard_map/all_gather | solution.py:98
  97.8 6.7 %fusion.46 = f32[128,2048]{0,1:T(8,128)S(1)} fusion(bf16[128,3072]{1,0:T(8,128)(2,1)S(1)} %all_gather.31, bf16[2048,3072]{1,0:T(8,128)(2,1)} %param.24), kind=kOutput, calls=%fused_computation.104 | convolution fusion | flops 1610612736 | bytes 14417920 | tf_op jit(solution)/shard_map/dot_general | solution.py:99
  104.6 1.7 copy.90
  106.3 1.8 fusion.5
  108.8 1.5 fusion.15
  110.3 5.7 %all-gather.7.cloned.1.call-done = f32[64,128,128]{2,1,0:T(8,128)} async-done(((f32[16,128,128]{2,1,0:T(8,128)}), f32[64,128,128]{2,1,0:T(8,128)}) %all-gather.7.cloned.1.call-update) | async-done | bytes 4194320 | tf_op jit(solution)/shard_map/all_gather | solution.py:15
  116.0 16.2 %while.36 = (s32[]{:T(128)}, f32[16,128,128]{2,1,0:T(8,128)S(1)}, f32[1]{0:T(128)}, s32[]{:T(128)}, f32[4,1]{0,1:T(1,128)S(1)}, /*index=5*/f32[4,16,128,128]{3,2,1,0:T(8,128)}, s32[]{:T(128)}, s32[]{:T(128)}, f32[]{:T(128)}) while((s32[]{:T(128)}, f32[16,128,128]{2,1,0:T(8,128)S(1)}, f32[1]{0:T(128)}, s32[]{:T(128)}, ...), condition=%wide.region_4.8_spmd.clone, body=%wide.region_3.7_spmd.clone.sunk | while | flops 1310728 | bytes 3145919 | solution.py:26
  118.2 1.8 select_select_fusion.4
  122.3 1.8 select_select_fusion.4
  126.4 1.8 select_select_fusion.4
  130.4 1.8 select_select_fusion.4
  132.2 2.5 multiply_reduce_fusion
  134.7 1.6 add_add_fusion
  136.4 3.3 fusion.10
  140.0 12.3 %convolution_bitcast_fusion = f32[3072,2048]{0,1:T(8,128)} fusion(bf16[128,2048]{0,1:T(8,128)(2,1)S(1)} %bitcast.153, bf16[128,3072]{1,0:T(8,128)(2,1)} %copy-done.7), kind=kOutput, calls=%fused_computation.12 | convolution fusion | flops 1610612736 | bytes 26476544 | tf_op jit(solution)/shard_map/dot_general | solution.py:128
  152.3 24.9 %copy.88 = f32[3072,2048]{1,0:T(8,128)} copy(f32[3072,2048]{0,1:T(8,128)} %convolution_bitcast_fusion) | data formatting | bytes 50331648
  177.2 2.0 copy.77
  179.2 1.6 fusion.6
  180.8 1.7 fusion.47
  182.5 2.0 fusion.7
  184.5 2.3 copy.78
  186.8 2.5 fusion.48
  189.3 2.5 fusion.30
  191.8 19.1 %while.37 = (s32[]{:T(128)}, f32[16,128,128]{2,1,0:T(8,128)S(1)}, f32[1]{0:T(128)}, s32[]{:T(128)}, f32[4,1]{0,1:T(1,128)S(1)}, /*index=5*/f32[4,16,128,128]{3,2...) while((s32[]{:T(128)}, f32[16,128,128]{2,1,0:T(8,128)S(1)}, ...), condition=%wide.region_8.12_spmd.clone, body=%wide.region_7.11_spmd.clone.sunk | while | flops 1310732 | bytes 3145981 | solution.py:26
  194.5 2.1 select_select_fusion.5
  199.3 1.9 select_select_fusion.5
  204.0 2.1 select_select_fusion.5
  208.8 2.1 select_select_fusion.5
  210.9 3.3 fusion.8
  214.2 2.0 copy.79
  216.2 2.0 fusion.9
  218.3 1.0 copy.80
  219.3 201.5 %reduce-scatter.4.cloned.1.call-done = f32[192,2048]{1,0:T(8,128)} async-done(((f32[3072,2048]{1,0:T(8,128)}), f32[192,2048]{1,0:T(8,128)}) %reduce-scatter.4.cloned.1.call-update) | async-done | bytes 1572880
  (81 shorter events, 14.4 us)
Async XLA Ops:
  7.2 2.6 copy-start
  7.2 34.8 %copy-start.17 = (u32[32]{0:T(128)S(1)}, u32[32]{0:T(128)}, u32[]{:S(2)}) copy-start(u32[32]{0:T(128)} %constant.228) | copy-start | bytes 388
  7.2 35.4 %copy-start.15 = (s32[4,4]{1,0:T(4,128)S(1)}, s32[4,4]{1,0:T(4,128)}, u32[]{:S(2)}) copy-start(s32[4,4]{1,0:T(4,128)} %param.21) | copy-start | bytes 196
  7.2 6.4 %copy-start.2 = (bf16[128,2048]{1,0:T(8,128)(2,1)S(1)}, bf16[128,2048]{1,0:T(8,128)(2,1)}, u32[]{:S(2)}) copy-start(bf16[128,2048]{1,0:T(8,128)(2,1)} %param.20) | copy-start | bytes 1572868
  9.8 55.4 %copy-start.16 = (s32[1,128]{1,0:T(1,128)S(1)}, s32[1,128]{1,0:T(1,128)}, u32[]{:S(2)}) copy-start(s32[1,128]{1,0:T(1,128)} %param.22) | copy-start | bytes 1540
  36.6 49.4 %copy-start.13 = (bf16[128,1536]{1,0:T(8,128)(2,1)S(1)}, bf16[128,1536]{1,0:T(8,128)(2,1)}, u32[]{:S(2)}) copy-start(bf16[128,1536]{1,0:T(8,128)(2,1)} %param.25) | copy-start | bytes 1179652
  36.6 18.6 %all-to-all-start = ((bf16[4,40,2048]{2,1,0:T(8,128)(2,1)}), bf16[4,40,2048]{2,1,0:T(8,128)(2,1)S(1)}, u32[]{:S(2)}, u32[]{:S(2)}) async-start(bf16[4,40,2048]{2,1,0:T(8,128)(2,1)} %bitcast.156), calls=%async_computation | async-start | bytes 1310720 | tf_op jit(solution)/shard_map/all_to_all | solution.py:63
  55.2 20.3 %all-to-all-start.2 = ((bf16[4,40,2048]{2,1,0:T(8,128)(2,1)}), bf16[4,40,2048]{2,1,0:T(8,128)(2,1)S(1)}, u32[]{:S(2)}, u32[]{:S(2)}) async-start(bf16[4,40,2048]{2,1,0:T(8,128)(2,1)} %bitcast.155), calls=%async_computation.2 | async-start | bytes 1310720 | tf_op jit(solution)/shard_map/all_to_all | solution.py:62
  61.9 54.1 %all-gather.7.cloned.1.call-start = ((), (), s32[]{:S(2)}) async-start(), calls=%async_computation.4 | async-start | bytes 5242880 | tf_op jit(solution)/shard_map/all_gather | solution.py:15
  77.6 30.4 %copy-start.4 = (bf16[16,16,8,128]{3,2,1,0:T(8,128)(2,1)}, bf16[16,16,8,128]{3,2,1,0:T(8,128)(2,1)S(1)}, u32[]{:S(2)}) copy-start(bf16[16,16,8,128]{3,2,1,0:T(8,128)(2,1)S(1)} %get-tuple-element.400) | copy-start | bytes 1572868
  78.2 26.3 %copy-start.10 = (bf16[128,16,128]{0,2,1:T(8,128)(2,1)}, bf16[128,16,128]{0,2,1:T(8,128)(2,1)S(1)}, u32[]{:S(2)}) copy-start(bf16[128,16,128]{0,2,1:T(8,128)(2,1)S(1)} %copy.62) | copy-start | bytes 1572868
  79.6 112.2 %all-gather.9.cloned.1.call-start = ((), (), s32[]{:S(2)}) async-start(), calls=%async_computation.5 | async-start | bytes 5242880 | tf_op jit(solution)/shard_map/all_gather | solution.py:15
  97.7 6.8 %copy-start.7 = (bf16[128,3072]{1,0:T(8,128)(2,1)}, bf16[128,3072]{1,0:T(8,128)(2,1)S(1)}, u32[]{:S(2)}) copy-start(bf16[128,3072]{1,0:T(8,128)(2,1)S(1)} %all_gather.31) | copy-start | bytes 2359300
  104.5 30.2 %copy-start.6 = (f32[128,2048]{0,1:T(8,128)}, f32[128,2048]{0,1:T(8,128)S(1)}, u32[]{:S(2)}) copy-start(f32[128,2048]{0,1:T(8,128)S(1)} %fusion.46) | copy-start | bytes 3145732
  104.5 27.7 %copy-start.14 = (f32[2048]{0:T(1024)S(1)}, f32[2048]{0:T(1024)}, u32[]{:S(2)}) copy-start(f32[2048]{0:T(1024)} %param.23) | copy-start | bytes 24580
  106.3 30.1 %copy-start.3 = (bf16[128,2048]{0,1:T(8,128)(2,1)}, bf16[128,2048]{0,1:T(8,128)(2,1)S(1)}, u32[]{:S(2)}) copy-start(bf16[128,2048]{0,1:T(8,128)(2,1)S(1)} %copy.90) | copy-start | bytes 1572868
  108.0 0.8 copy-start.9
  136.4 15.9 %copy-start.8 = (bf16[128,16,128]{0,2,1:T(8,128)(2,1)}, bf16[128,16,128]{0,2,1:T(8,128)(2,1)S(1)}, u32[]{:S(2)}) copy-start(bf16[128,16,128]{0,2,1:T(8,128)(2,1)S(1)} %get-tuple-element.387) | copy-start | bytes 1572868
  139.7 281.1 %reduce-scatter.4.cloned.1.call-start = ((), (), s32[]{:S(2)}) async-start(), calls=%async_computation.6 | async-start | bytes 26738688
  180.8 3.7 copy-start.11
  184.5 26.4 %copy-start.5 = (bf16[16,16,8,128]{3,2,1,0:T(8,128)(2,1)S(1)}, bf16[16,16,8,128]{3,2,1,0:T(8,128)(2,1)}, u32[]{:S(2)}) copy-start(bf16[16,16,8,128]{3,2,1,0:T(8,128)(2,1)} %copy-done.4) | copy-start | bytes 1572868
  189.3 231.5 %copy-start.1 = (bf16[128,2048]{1,0:T(8,128)(2,1)S(1)}, bf16[128,2048]{1,0:T(8,128)(2,1)}, u32[]{:S(2)}) copy-start(bf16[128,2048]{1,0:T(8,128)(2,1)} %param.19) | copy-start | bytes 1572868
  191.8 24.4 %copy-start.12 = (f32[16,128,128]{2,1,0:T(8,128)S(1)}, f32[16,128,128]{2,1,0:T(8,128)}, u32[]{:S(2)}) copy-start(f32[16,128,128]{2,1,0:T(8,128)} %fusion.30) | copy-start | bytes 3145732
Sparse Core Ops, SparseCore 0:
  79.7 36.2 all-gather.6
  139.8 34.4 all-gather.8
  179.0 241.8 reduce-scatter.3
where the time goes:
time: 433 us; the launch traced here: 427 us
  waiting for transfers between devices  225 us (52%)
  local copies, waits for them, and re-layouts  51.2 us (12%)
  matrix products  45 us (10%)
  blocking collectives  38 us (9%)
  other arithmetic  26 us (6%)
  loops' own time  15.1 us (3%)
  between operations  14.1 us (3%)
  starting transfers between devices  12.4 us (3%)
    unnamed x4, waiting for transfers between devices  202 us
    unnamed x46, local copies, waits for them, and re-layouts  34.5 us
    all_to_all x1, blocking collectives, local(): lax.all_to_all(packed[0], 'dp', split_axis=0, concat_axis=0, tiled=True)  20.6 us
    select_n x8, other arithmetic, lap(): return jax.tree.map(lambda a, b: jnp.where(reached, a, b), new, before)  15.2 us
    another operation x2, loops' own time, prefix(): return lax.fori_loop(0, peers, lap, start)  15.1 us
    all_to_all x1, waiting for transfers between devices, local(): lax.all_to_all(packed[2], 'dp', split_axis=0, concat_axis=0, tiled=True)  12.3 us
    dot_general x1, matrix products, local(): lax.dot_general(full_grad, normed, (((0,), (0,)), ((), ())), preferred_el...  12.3 us
    all_gather x1, blocking collectives, local(): full_grad = lax.all_gather(out_grad, 'mp', axis=1, tiled=True)  11.7 us
  transfers between devices with their start and end apart: 5, of which 4 were waited for; matrix products, arithmetic and copies ran while one was open for 22% of the time, Pallas kernels for 0%

commit v1 on v0

v1 whole, which is shorter than its diff:
```python
import functools

import jax
import jax.numpy as jnp
from jax import lax
from jax.experimental import pallas as pl
from jax.experimental.pallas import tpu as pltpu
from jax.sharding import PartitionSpec as P

HS = 128


NORM_EPS = 1e-06
F32 = jnp.float32
BF16 = jnp.bfloat16


def mm(a, b, ca, cb):
    return lax.dot_general(a, b, (((ca,), (cb,)), ((), ())), preferred_element_type=F32)


def place_body(blocks, pick_ref, tail_ref, aq_ref, ak_ref, av_ref, q_ref, k_ref, v_ref, st_ref):
    pick = pick_ref[...]
    tail = tail_ref[...]
    for src, dst in ((aq_ref, q_ref), (ak_ref, k_ref), (av_ref, v_ref)):
        dst[...] = mm(pick, src[...], 1, 0).astype(BF16)
    for h in range(blocks):
        cols = slice(h * HS, (h + 1) * HS)
        st_ref[:, cols] = mm(k_ref[:, cols] * tail, v_ref[:, cols], 0, 0)


def forward_body(
    blocks, doc_ref, carried_ref, headp_ref, gain_ref, q_ref, k_ref, v_ref, st_ref, dn_ref,
    normed_ref, dh_ref, r_ref,
):
    doc = doc_ref[...]
    carried = carried_ref[...]
    headp = headp_ref[...]
    for h in range(blocks):
        cols = slice(h * HS, (h + 1) * HS)
        q, k, v = q_ref[:, cols], k_ref[:, cols], v_ref[:, cols]
        p = (mm(q, k, 1, 1) * doc).astype(BF16)
        attn = mm(p, v, 1, 0) + mm(q, st_ref[:, cols], 1, 0) * carried
        gain = gain_ref[:, cols]
        scale = lax.rsqrt(jnp.mean(attn * attn, axis=-1, keepdims=True) + NORM_EPS)
        unit = attn * scale
        normed_ref[:, cols] = (unit * gain).astype(BF16)
        g = dn_ref[:, cols] * gain
        d_attn = scale * (g - unit * jnp.mean(g * unit, axis=-1, keepdims=True))
        d_half = d_attn.astype(BF16)
        dh_ref[:, cols] = d_half
        r_ref[:, cols] = mm(q * headp, d_half, 0, 0)


def backward_body(
    blocks, doc_ref, carried_ref, rev_ref, q_ref, k_ref, v_ref, d_ref, st_ref, rst_ref,
    dq_ref, dk_ref, dv_ref,
):
    doc = doc_ref[...]
    carried = carried_ref[...]
    rev = rev_ref[...]
    for h in range(blocks):
        cols = slice(h * HS, (h + 1) * HS)
        q, k, v, d = q_ref[:, cols], k_ref[:, cols], v_ref[:, cols], d_ref[:, cols]
        st, rst = st_ref[:, cols], rst_ref[:, cols]
        p = (mm(q, k, 1, 1) * doc).astype(BF16)
        dp = (mm(d, v, 1, 1) * doc).astype(BF16)
        dq_ref[:, cols] = (mm(dp, k, 1, 0) + mm(d, st, 1, 1) * carried).astype(BF16)
        dk_ref[:, cols] = (mm(dp, q, 0, 0) + mm(v, rst, 1, 1) * rev).astype(BF16)
        dv_ref[:, cols] = (mm(p, d, 0, 0) + mm(k, rst, 1, 0) * rev).astype(BF16)


def by_heads(body, heads, fixed, moving, outs):
    blocks = 4 if heads % 4 == 0 else 1
    span = blocks * HS
    rows_of = lambda a: pl.BlockSpec((a.shape[0], span), lambda i: (0, i))
    whole = lambda a: pl.BlockSpec(a.shape, lambda i: (0, 0))
    moved = sum(a.size * a.dtype.itemsize for a in (*fixed, *moving, *outs))
    return pl.pallas_call(
        functools.partial(body, blocks),
        grid=(heads // blocks,),
        in_specs=[whole(a) for a in fixed] + [rows_of(a) for a in moving],
        out_specs=[rows_of(a) for a in outs],
        out_shape=list(outs),
        cost_estimate=pl.CostEstimate(
            flops=16 * heads * HS * HS * HS, bytes_accessed=moved, transcendentals=0
        ),
    )(*fixed, *moving)


def chain(local, ids, axis, reverse):
    peers, place = lax.axis_size(axis), lax.axis_index(axis)
    step = -1 if reverse else 1
    before = jnp.take(ids, jnp.clip(place - step, 0, peers - 1))
    joined = before == jnp.take(ids, place)
    got = jnp.zeros(local.shape, BF16)
    for hop in range(peers - 1):
        at = peers - 1 - hop if reverse else hop
        sent = local if hop == 0 else local + jnp.where(joined, got.astype(F32), 0.0)
        got = got + lax.ppermute(sent.astype(BF16), axis, [(at, at + step)])
    first = place == (peers - 1 if reverse else 0)
    return got, jnp.where(first, jnp.full_like(before, -1.0), before)


def local(queries, key_rows, value_rows, row_plan, segments, norm_gain, out_weight, out_grad):
    row_total = queries.shape[0]
    width = queries.shape[1]
    heads = width // HS
    groups = lax.axis_size("dp")
    my_group = lax.axis_index("dp")
    devices = groups * lax.axis_size("seq")
    capacity = row_total // min(groups, 8) + row_total // 16
    slots_all = groups * capacity
    send_start = jnp.cumsum(row_plan, axis=1) - row_plan
    recv_start = jnp.cumsum(row_plan, axis=0) - row_plan
    slots = jnp.arange(capacity, dtype=jnp.int32)
    positions = jnp.arange(row_total, dtype=jnp.int32)
    my_send = jnp.take(send_start, my_group, axis=0)
    send_index = jnp.minimum(my_send[:, None] + slots[None, :], row_total - 1).reshape(-1)
    send_hot = (send_index[:, None] == positions[None, :]).astype(BF16)

    def hand(x):
        packed = jnp.dot(send_hot, x, preferred_element_type=F32).astype(BF16)
        return lax.all_to_all(packed, "dp", split_axis=0, concat_axis=0, tiled=True)

    arrived = (hand(queries), hand(key_rows), hand(value_rows))
    my_start = jnp.take(recv_start, my_group, axis=1)
    my_end = my_start + jnp.take(row_plan, my_group, axis=1)
    source = jnp.sum((my_end[None, :] <= positions[:, None]).astype(jnp.int32), axis=1)
    pick = source * capacity + positions - jnp.take(my_start, source)
    pick_hot = (pick[:, None] == jnp.arange(slots_all, dtype=jnp.int32)[None, :]).astype(BF16)

    seg_f = segments[0].astype(F32)
    edges = lax.all_gather(jnp.stack([seg_f[0], seg_f[-1]]), "seq")
    causal = positions[None, :] <= positions[:, None]
    same_doc = (causal & (seg_f[:, None] == seg_f[None, :])).astype(F32)
    tail = (seg_f == seg_f[-1]).astype(BF16)[:, None]
    head_part = (seg_f == seg_f[0]).astype(BF16)[:, None]

    full_grad = lax.all_gather(out_grad, "mp", axis=1, tiled=True)
    d_normed = lax.dot_general(
        full_grad, out_weight, (((1,), (1,)), ((), ())), preferred_element_type=F32
    )
    grad_cols = full_grad.T.reshape(devices, full_grad.shape[1] // devices, row_total)
    grad_cols = lax.all_to_all(grad_cols, ("dp", "seq"), split_axis=0, concat_axis=0, tiled=True)

    half = jax.ShapeDtypeStruct((row_total, width), BF16)
    state = jax.ShapeDtypeStruct((HS, width), F32)
    q, k, v, local_state = by_heads(
        place_body, heads, (pick_hot, tail), arrived, (half, half, half, state)
    )
    state_in, id_in = chain(local_state, edges[:, 1], "seq", False)
    carried = (seg_f == id_in).astype(F32)[:, None]
    gain_row = norm_gain.reshape(1, width)
    normed, d_half, local_r = by_heads(
        forward_body,
        heads,
        (same_doc, carried, head_part),
        (gain_row, q, k, v, state_in, d_normed),
        (half, half, state),
    )
    everyone = lax.all_gather(normed, ("dp", "seq"), axis=0)
    rstate_in, rid_in = chain(local_r, edges[:, 0], "seq", True)
    rev_use = (seg_f == rid_in).astype(F32)[:, None]
    dquery, dkey, dvalue = by_heads(
        backward_body,
        heads,
        (same_doc, carried, rev_use),
        (q, k, v, d_half, state_in, rstate_in),
        (half, half, half),
    )
    weight_grad = lax.dot_general(
        grad_cols, everyone, (((0, 2), (0, 1)), ((), ())), preferred_element_type=F32
    )
    return normed, dquery, dkey, dvalue, weight_grad


def solution(mesh):
    placed = (
        P(("dp", "seq"), "mp"),
        P(("dp", "seq"), "mp"),
        P(("dp", "seq"), "mp"),
        P(),
        P("dp", "seq"),
        P("mp"),
        P("mp", None),
        P(("dp", "seq"), "mp"),
    )
    return jax.shard_map(
        local,
        mesh=mesh,
        in_specs=placed,
        out_specs=(
            P(("dp", "seq"), "mp"),
            P(("dp", "seq"), "mp"),
            P(("dp", "seq"), "mp"),
            P(("dp", "seq"), "mp"),
            P(("dp", "seq"), "mp"),
        ),
        check_vma=False,
    )
```

time: 433 us -> 223 us (0.52)
  waiting for transfers between devices: 225 us -> 80.3 us
  local copies, waits for them, and re-layouts: 51.2 us -> 8.18 us
  matrix products: 45 us -> 21.2 us
  starting transfers between devices: 12.4 us -> 33.5 us
  Pallas kernels: 0 us -> 19.8 us
  blocking collectives: 38 us -> 18.2 us
  loops' own time: 15.1 us -> 0 us
    unnamed x4 -> x1, waiting for transfers between devices: 202 us -> 0.02 us
    all_gather x2 -> x1, waiting for transfers between devices: 5.68 us -> 43.3 us  [local(): everyone = lax.all_gather(normed, ('dp', 'seq'), axis=0)]
    unnamed x46 -> x12, local copies, waits for them, and re-layouts: 34.5 us -> 2.09 us
    dot_general x13 -> x4, matrix products: 38.3 us -> 11.4 us  [the longest x3 5.73 us: hand(): packed = jnp.dot(send_hot, x, preferred_element_type=F32).astype(BF16)]
    all_to_all x1 -> x0, blocking collectives: 20.6 us -> none  [local(): lax.all_to_all(packed[0], 'dp', split_axis=0, concat_axis=0, tiled=True)]
    pallas_call x0 -> x3, Pallas kernels: none -> 19.8 us  [by_heads(): pl.pallas_call(functools.partial(body, blocks), grid=(heads // blocks,),...]
    select_n x10 -> x0, other arithmetic: 16.5 us -> none  [the longest x8 15.2 us: lap(): return jax.tree.map(lambda a, b: jnp.where(reached, a, b), new, before)]
    all_to_all x2 -> x4, starting transfers between devices: 12.1 us -> 27.3 us  [the longest x3 18.8 us: hand(): return lax.all_to_all(packed, 'dp', split_axis=0, concat_axis=0, tiled=True)]
  transfers between devices with their start and end apart: 5 -> 11, of which waited for: 4 -> 7; matrix products, arithmetic and copies ran while one was open for 22% -> 16% of each run, Pallas kernels for 0% -> 3%
where the time goes in v1:
time: 223 us; the launch traced here: 220 us
  waiting for transfers between devices  80.3 us (36%)
  starting transfers between devices  33.5 us (15%)
  other arithmetic  21.7 us (10%)
  matrix products  21.2 us (10%)
  Pallas kernels  19.8 us (9%)
  blocking collectives  18.2 us (8%)
  between operations  17.3 us (8%)
  local copies, waits for them, and re-layouts  8.18 us (4%)
    all_gather x1, waiting for transfers between devices, local(): everyone = lax.all_gather(normed, ('dp', 'seq'), axis=0)  43.3 us
    pallas_call x3, Pallas kernels, by_heads(): pl.pallas_call(functools.partial(body, blocks), grid=(heads // blocks,),...  19.8 us
    all_to_all x3, starting transfers between devices, hand(): return lax.all_to_all(packed, 'dp', split_axis=0, concat_axis=0, tiled=True)  18.8 us
    all_to_all x3, waiting for transfers between devices, hand(): return lax.all_to_all(packed, 'dp', split_axis=0, concat_axis=0, tiled=True)  16.7 us
    all_to_all x1, waiting for transfers between devices, local(): lax.all_to_all(grad_cols, ('dp', 'seq'), split_axis=0, concat_axis=0, til...  12.3 us
    all_gather x1, blocking collectives, local(): full_grad = lax.all_gather(out_grad, 'mp', axis=1, tiled=True)  12.2 us
    dot_general x1, matrix products, local(): lax.dot_general(full_grad, out_weight, (((1,), (1,)), ((), ())), preferre...  9.8 us
    all_to_all x1, starting transfers between devices, local(): lax.all_to_all(grad_cols, ('dp', 'seq'), split_axis=0, concat_axis=0, til...  8.57 us
  transfers between devices with their start and end apart: 11, of which 7 were waited for; matrix products, arithmetic and copies ran while one was open for 16% of the time, Pallas kernels for 3%

profile of v1, /device:TPU:12, one launch (start us, length us, event | category | flops | bytes accessed | tf_op | source)
XLA Modules:
  0.0 220.1 jit_solution(12133292273872337727)
XLA Ops:
  7.2 0.8 reduce_window_sum.22
  8.0 0.9 reduce_window_sum.23
  9.7 1.2 convolution_convert_fusion.2
  10.9 5.3 %all-to-all-start = ((bf16[4,40,2048]{2,1,0:T(8,128)(2,1)}), bf16[4,40,2048]{2,1,0:T(8,128)(2,1)S(1)}, u32[]{:S(2)}, u32[]{:S(2)}) async-start(bf16[4,40,2048]{2,1,0:T(8,128)(2,1)} %bitcast.20), calls=%async_computation | async-start | bytes 1310720 | tf_op jit(solution)/shard_map/all_to_all | solution.py:124
  16.2 2.3 %convolution_convert_fusion.1 = bf16[160,2048]{1,0:T(8,128)(2,1)} fusion(bf16[128,2048]{1,0:T(8,128)(2,1)} %param.11, s32[160]{0:T(256)S(1)} %min.23), kind=kOutput, calls=%fused_computation.2 | convolution fusion | flops 84234240 | bytes 1180288 | tf_op jit(solution)/shard_map/dot_general | solution.py:123
  18.5 11.8 %all-to-all-done = bf16[4,40,2048]{2,1,0:T(8,128)(2,1)S(1)} async-done(((bf16[4,40,2048]{2,1,0:T(8,128)(2,1)}), bf16[4,40,2048]{2,1,0:T(8,128)(2,1)S(1)}, u32[]{:S(2)}, u32[]{:S(2)}) %all-to-all-start) | async-done | bytes 655392 | tf_op jit(solution)/shard_map/all_to_all | solution.py:124
  30.3 6.7 %all-to-all-start.1 = ((bf16[4,40,2048]{2,1,0:T(8,128)(2,1)}), bf16[4,40,2048]{2,1,0:T(8,128)(2,1)S(1)}, u32[]{:S(2)}, u32[]{:S(2)}) async-start(bf16[4,40,2048]{2,1,0:T(8,128)(2,1)} %bitcast.22), calls=%async_computation.1 | async-start | bytes 1310720 | tf_op jit(solution)/shard_map/all_to_all | solution.py:124
  37.0 1.2 dynamic-slice.25
  40.1 1.5 maximum_dynamic-update-slice_fusion
  41.6 5.9 %all-reduce = f32[8]{0:T(128)S(1)} all-reduce(f32[8]{0:T(128)S(1)} %maximum_dynamic-update-slice_fusion), channel_id=2, replica_groups=mesh['dp'=4,'seq'=4,'mp'=2] {'seq'}, use_global_device_ids=true, to_apply=%add | all-reduce | flops 8 | bytes 64
  47.6 2.2 %convolution_convert_fusion = bf16[160,2048]{1,0:T(8,128)(2,1)} fusion(bf16[128,2048]{1,0:T(8,128)(2,1)} %param.12, s32[160]{0:T(256)S(1)} %min.23), kind=kOutput, calls=%fused_computation.1 | convolution fusion | flops 84234240 | bytes 1180288 | tf_op jit(solution)/shard_map/dot_general | solution.py:123
  49.8 0.7 all-to-all-done.1
  50.6 6.7 %all-to-all-start.2 = ((bf16[4,40,2048]{2,1,0:T(8,128)(2,1)}), bf16[4,40,2048]{2,1,0:T(8,128)(2,1)S(1)}, u32[]{:S(2)}, u32[]{:S(2)}) async-start(bf16[4,40,2048]{2,1,0:T(8,128)(2,1)} %bitcast.24), calls=%async_computation.2 | async-start | bytes 1310720 | tf_op jit(solution)/shard_map/all_to_all | solution.py:124
  59.1 2.0 fusion.11
  61.1 0.7 copy.25.tail_ref
  61.8 0.9 select_reduce_fusion
  63.5 2.5 %fusion.9 = s32[128]{0:T(128)S(1)} fusion(s32[128]{0:T(128)S(1)} %convert_reduce_fusion, s32[]{:T(128)} %bitcast.12, s32[]{:T(128)} %bitcast.13, s32[]{:T(128)} %bitcast.15, s32[]{:T(128)} %bitcast.14), kind=kLoop, calls=%fused_computation.41 | loop fusion | flops 2432 | bytes 1040 | tf_op jit(solution)/shard_map/sub | solution.py:130
  66.0 0.7 fusion.pick_ref
  66.7 4.2 %all-to-all-done.2 = bf16[4,40,2048]{2,1,0:T(8,128)(2,1)S(1)} async-done(((bf16[4,40,2048]{2,1,0:T(8,128)(2,1)}), bf16[4,40,2048]{2,1,0:T(8,128)(2,1)S(1)}, u32[]{:S(2)}, u32[]{:S(2)}) %all-to-all-start.2) | async-done | bytes 655392 | tf_op jit(solution)/shard_map/all_to_all | solution.py:124
  70.9 0.8 copy-done.3
  71.7 4.6 %shard_map.119 = (bf16[128,2048]{1,0:T(8,128)(2,1)}, bf16[128,2048]{1,0:T(8,128)(2,1)}, bf16[128,2048]{1,0:T(8,128)(2,1)}, f32[128,2048]{1,0:T(8,128)}) custom-call(bf16[128,160]{1,0:T(8,128)(2,1)} %fusion.pick_ref, bf16[128,1]{1,0:T(8,128)(2,1)} %copy.25.tail_ref, bf16[160,2048]{1,0:T(8,128)(2,1)} %bitcast.60, bf16[160,2048]{1,0:T(8,128)(2,1)} %bitcast.61, ...), custom_call_target="tpu_custom_call" | custom-call | flops 536870912 | bytes 4628736 | tf_op jit(solution)/shard_map/pallas_call | solution.py:79
  76.3 1.3 convert_element_type.145
  77.6 1.3 collective-permute-start
  79.5 0.9 collective-permute-done
  80.4 1.4 add_convert_fusion.3
  81.8 0.7 collective-permute-start.1
  82.5 0.7 copy.26.carried_ref
  83.2 0.7 copy.27.headp_ref
  83.9 12.2 %all_gather.17 = bf16[128,3072]{1,0:T(8,128)(2,1)S(1)} all-gather(bf16[128,1536]{1,0:T(8,128)(2,1)S(1)} %copy-done.4), channel_id=1, replica_groups=mesh['dp'=4,'seq'=4,'mp'=2] {'mp'}, dimensions={1}, use_global_device_ids=true | all-gather | bytes 1179648 | tf_op jit(solution)/shard_map/all_gather | solution.py:140
  96.2 0.7 fusion.2.doc_ref
  96.9 1.5 add_convert_fusion.2
  99.1 9.8 %fusion.18.dn_ref = f32[128,2048]{1,0:T(8,128)} fusion(bf16[128,3072]{1,0:T(8,128)(2,1)S(1)} %all_gather.17, bf16[2048,3072]{1,0:T(8,128)(2,1)} %param.16), kind=kOutput, calls=%fused_computation.52 | convolution fusion | flops 1610612736 | bytes 14417920 | tf_op jit(solution)/shard_map/dot_general | solution.py:141
  108.9 0.9 add.106.st_ref
  109.8 8.8 %shard_map.120 = (bf16[128,2048]{1,0:T(8,128)(2,1)}, bf16[128,2048]{1,0:T(8,128)(2,1)}, f32[128,2048]{1,0:T(8,128)}) custom-call(f32[128,128]{1,0:T(8,128)} %fusion.2.doc_ref, f32[128,1]{1,0:T(8,128)} %copy.26.carried_ref, bf16[128,1]{1,0:T(8,128)(2,1)} %copy.27.headp_ref, f32[1,2048]{1,0:T(1,128)} %bitcast.63, bf16[128,2048]{1,0:T(8,128)(2,1)} %get-tuple-element.16.q_ref, ...), custom_call_target="tpu_custom_call" | custom-call | flops 536870912 | bytes 5317376 | tf_op jit(solution)/shard_map/pallas_call | solution.py:79
  118.6 1.3 convert_element_type.152
  121.1 1.4 add_convert_fusion.1
  122.5 1.5 collective-permute-start.4
  124.0 1.2 copy.30
  125.1 8.6 %all-to-all-start.3 = ((bf16[16,192,128]{2,1,0:T(8,128)(2,1)}), bf16[16,192,128]{2,1,0:T(8,128)(2,1)S(1)}, u32[]{:S(2)}, u32[]{:S(2)}) async-start(bf16[16,192,128]{2,1,0:T(8,128)(2,1)} %bitcast.37), calls=%async_computation.3 | async-start | bytes 1572864 | tf_op jit(solution)/shard_map/all_to_all | solution.py:145
  133.7 1.6 add_convert_fusion
  135.3 1.3 collective-permute-start.5
  136.6 0.7 copy.29.rev_ref
  137.4 7.2 %collective-permute-done.5 = bf16[128,2048]{1,0:T(8,128)(2,1)S(1)} collective-permute-done((bf16[128,2048]{1,0:T(8,128)(2,1)S(1)}, bf16[128,2048]{1,0:T(8,128)(2,1)S(1)}, u32[]{:S(2)}, u32[]{:S(2)}) %collective-permute-start.5) | collective-permute-done | bytes 524320 | tf_op jit(solution)/shard_map/ppermute | solution.py:100
  144.5 1.0 add.110.rst_ref
  145.5 6.5 %shard_map.121 = (bf16[128,2048]{1,0:T(8,128)(2,1)}, bf16[128,2048]{1,0:T(8,128)(2,1)}, bf16[128,2048]{1,0:T(8,128)(2,1)}) custom-call(f32[128,128]{1,0:T(8,128)} %fusion.2.doc_ref, f32[128,1]{1,0:T(8,128)} %copy.26.carried_ref, f32[128,1]{1,0:T(8,128)} %copy.29.rev_ref, bf16[128,2048]{1,0:T(8,128)(2,1)} %get-tuple-element.16.q_ref, ...), custom_call_target="tpu_custom_call" | custom-call | flops 536870912 | bytes 4785152 | tf_op jit(solution)/shard_map/pallas_call | solution.py:79
  152.0 12.3 %all-to-all-done.3 = bf16[16,192,128]{2,1,0:T(8,128)(2,1)S(1)} async-done(((bf16[16,192,128]{2,1,0:T(8,128)(2,1)}), bf16[16,192,128]{2,1,0:T(8,128)(2,1)S(1)}, u32[]{:S(2)}, u32[]{:S(2)}) %all-to-all-start.3) | async-done | bytes 786464 | tf_op jit(solution)/shard_map/all_to_all | solution.py:145
  164.3 43.3 %all-gather.4.cloned.1.call-done = bf16[2048,2048]{1,0:T(8,128)(2,1)} async-done(((bf16[128,2048]{1,0:T(8,128)(2,1)}), bf16[2048,2048]{1,0:T(8,128)(2,1)}) %all-gather.4.cloned.1.call-update) | async-done | bytes 8388624 | tf_op jit(solution)/shard_map/all_gather | solution.py:162
  207.6 5.7 %convolution_bitcast_fusion = f32[192,2048]{1,0:T(8,128)} fusion(bf16[16,192,128]{2,1,0:T(8,128)(2,1)S(1)} %all-to-all-done.3, bf16[16,128,2048]{2,1,0:T(8,128)(2,1)} %bitcast.64), kind=kOutput, calls=%fused_computation | convolution fusion | flops 1610612736 | bytes 10747904 | tf_op jit(solution)/shard_map/dot_general | solution.py:172
  (30 shorter events, 5.0 us)
Async XLA Ops:
  7.2 2.5 %copy-start = (bf16[128,2048]{1,0:T(8,128)(2,1)S(1)}, bf16[128,2048]{1,0:T(8,128)(2,1)}, u32[]{:S(2)}) copy-start(bf16[128,2048]{1,0:T(8,128)(2,1)} %param.10) | copy-start | bytes 1572868
  7.2 76.8 %copy-start.4 = (bf16[128,1536]{1,0:T(8,128)(2,1)S(1)}, bf16[128,1536]{1,0:T(8,128)(2,1)}, u32[]{:S(2)}) copy-start(bf16[128,1536]{1,0:T(8,128)(2,1)} %param.17) | copy-start | bytes 1179652
  10.9 19.3 %all-to-all-start = ((bf16[4,40,2048]{2,1,0:T(8,128)(2,1)}), bf16[4,40,2048]{2,1,0:T(8,128)(2,1)S(1)}, u32[]{:S(2)}, u32[]{:S(2)}) async-start(bf16[4,40,2048]{2,1,0:T(8,128)(2,1)} %bitcast.20), calls=%async_computation | async-start | bytes 1310720 | tf_op jit(solution)/shard_map/all_to_all | solution.py:124
  30.2 40.6 %copy-start.1 = (bf16[4,40,2048]{2,1,0:T(8,128)(2,1)}, bf16[4,40,2048]{2,1,0:T(8,128)(2,1)S(1)}, u32[]{:S(2)}) copy-start(bf16[4,40,2048]{2,1,0:T(8,128)(2,1)S(1)} %all-to-all-done) | copy-start | bytes 1966084
  30.3 20.3 %all-to-all-start.1 = ((bf16[4,40,2048]{2,1,0:T(8,128)(2,1)}), bf16[4,40,2048]{2,1,0:T(8,128)(2,1)S(1)}, u32[]{:S(2)}, u32[]{:S(2)}) async-start(bf16[4,40,2048]{2,1,0:T(8,128)(2,1)} %bitcast.22), calls=%async_computation.1 | async-start | bytes 1310720 | tf_op jit(solution)/shard_map/all_to_all | solution.py:124
  50.6 20.3 %copy-start.2 = (bf16[4,40,2048]{2,1,0:T(8,128)(2,1)}, bf16[4,40,2048]{2,1,0:T(8,128)(2,1)S(1)}, u32[]{:S(2)}) copy-start(bf16[4,40,2048]{2,1,0:T(8,128)(2,1)S(1)} %all-to-all-done.1) | copy-start | bytes 1966084
  50.6 20.3 %all-to-all-start.2 = ((bf16[4,40,2048]{2,1,0:T(8,128)(2,1)}), bf16[4,40,2048]{2,1,0:T(8,128)(2,1)S(1)}, u32[]{:S(2)}, u32[]{:S(2)}) async-start(bf16[4,40,2048]{2,1,0:T(8,128)(2,1)} %bitcast.24), calls=%async_computation.2 | async-start | bytes 1310720 | tf_op jit(solution)/shard_map/all_to_all | solution.py:124
  57.3 150.3 %all-gather.4.cloned.1.call-start = ((), (), s32[]{:S(2)}) async-start(), calls=%async_computation.4 | async-start | bytes 8912896 | tf_op jit(solution)/shard_map/all_gather | solution.py:162
  70.9 0.8 copy-start.3
  77.6 2.8 %collective-permute-start = (bf16[128,2048]{1,0:T(8,128)(2,1)S(1)}, bf16[128,2048]{1,0:T(8,128)(2,1)S(1)}, u32[]{:S(2)}, u32[]{:S(2)}) collective-permute-start(bf16[128,2048]{1,0:T(8,128)(2,1)S(1)} %convert_element_type.145), channel_id=1, source_target_pairs={{0,2},{1,3},{8,10},{9,11},{16,18},{17,19},{24,26},{25,27}} | collective-permute-start | bytes 1572872 | tf_op jit(solution)/shard_map/ppermute | solution.py:100
  81.8 15.1 %collective-permute-start.1 = (bf16[128,2048]{1,0:T(8,128)(2,1)S(1)}, bf16[128,2048]{1,0:T(8,128)(2,1)S(1)}, u32[]{:S(2)}, u32[]{:S(2)}) collective-permute-start(bf16[128,2048]{1,0:T(8,128)(2,1)S(1)} %add_convert_fusion.3), channel_id=1, source_target_pairs={{2,4},{3,5},{10,12},{11,13},{18,20},{19,21},{26,28},{27,29}} | collective-permute-start | bytes 1572872 | tf_op jit(solution)/shard_map/ppermute | solution.py:100
  98.4 10.5 %collective-permute-start.2 = (bf16[128,2048]{1,0:T(8,128)(2,1)S(1)}, bf16[128,2048]{1,0:T(8,128)(2,1)S(1)}, u32[]{:S(2)}, u32[]{:S(2)}) collective-permute-start(bf16[128,2048]{1,0:T(8,128)(2,1)S(1)} %get-tuple-element.94), channel_id=1, source_target_pairs={{4,6},{5,7},{12,14},{13,15},{20,22},{21,23},{28,30},{29,31}} | collective-permute-start | bytes 1572872 | tf_op jit(solution)/shard_map/ppermute | solution.py:100
  119.9 1.3 collective-permute-start.3
  122.5 11.2 %collective-permute-start.4 = (bf16[128,2048]{1,0:T(8,128)(2,1)S(1)}, bf16[128,2048]{1,0:T(8,128)(2,1)}, u32[]{:S(2)}, u32[]{:S(2)}) collective-permute-start(bf16[128,2048]{1,0:T(8,128)(2,1)S(1)} %add_convert_fusion.1), channel_id=1, source_target_pairs={{4,2},{5,3},{12,10},{13,11},{20,18},{21,19},{28,26},{29,27}} | collective-permute-start | bytes 1572872 | tf_op jit(solution)/shard_map/ppermute | solution.py:100
  125.1 39.1 %all-to-all-start.3 = ((bf16[16,192,128]{2,1,0:T(8,128)(2,1)}), bf16[16,192,128]{2,1,0:T(8,128)(2,1)S(1)}, u32[]{:S(2)}, u32[]{:S(2)}) async-start(bf16[16,192,128]{2,1,0:T(8,128)(2,1)} %bitcast.37), calls=%async_computation.3 | async-start | bytes 1572864 | tf_op jit(solution)/shard_map/all_to_all | solution.py:145
  135.3 9.2 %collective-permute-start.5 = (bf16[128,2048]{1,0:T(8,128)(2,1)S(1)}, bf16[128,2048]{1,0:T(8,128)(2,1)S(1)}, u32[]{:S(2)}, u32[]{:S(2)}) collective-permute-start(bf16[128,2048]{1,0:T(8,128)(2,1)S(1)} %get-tuple-element.92), channel_id=1, source_target_pairs={{2,0},{3,1},{10,8},{11,9},{18,16},{19,17},{26,24},{27,25}} | collective-permute-start | bytes 1572872 | tf_op jit(solution)/shard_map/ppermute | solution.py:100
Sparse Core Ops, SparseCore 0:
  118.7 88.8 all-gather.3

commit v2 on v1

--- a/solution.py
+++ b/solution.py
@@ -88,18 +88,220 @@
     )(*fixed, *moving)
 
 
-def chain(local, ids, axis, reverse):
+def gather_body(
+    n_z, n_s, grads_ref, normed_ref, local_ref, joined_ref, wg_ref, rst_ref,
+    buf, got, sent, zsend, zrecv, xsend, xrecv, csend, crecv, ksend, krecv, own_sem,
+):
+    n_x = n_s // 2
+    z, s = lax.axis_index("dp"), lax.axis_index("seq")
+    x, c = lax.div(s, 2), lax.rem(s, 2)
+    mate = 2 * x + 1 - c
+    width = normed_ref.shape[1]
+    span = 512 if width % 512 == 0 else HS
+
+    def remote(src, dst, ssem, rsem, target):
+        return pltpu.make_async_remote_copy(
+            src_ref=src, dst_ref=dst, send_sem=ssem, recv_sem=rsem,
+            device_id=target, device_id_type=pl.DeviceIdType.MESH,
+        )
+
+    def zcopy(up, zz, src):
+        return remote(src, buf.at[zz, s], zsend.at[0 if up else 1, zz], zrecv.at[zz],
+                      {"dp": z + 1 if up else z - 1})
+
+    def xcopy(zz, j, src):
+        peer = 2 * lax.rem(x + j, n_x) + c
+        return remote(src, buf.at[zz, s], xsend.at[zz, j], xrecv.at[zz, x], {"seq": peer})
+
+    def xland(zz, xs):
+        at = buf.at[zz, 2 * xs + c]
+        return remote(at, at, xsend.at[zz, 0], xrecv.at[zz, xs], {"seq": 2 * xs + c})
+
+    def ccopy(zz, xs, src):
+        return remote(src, buf.at[zz, 2 * xs + c], csend.at[zz, xs], crecv.at[zz, xs],
+                      {"seq": mate})
+
+    def cland(zz, xs):
+        at = buf.at[zz, 2 * xs + 1 - c]
+        return remote(at, at, csend.at[zz, xs], crecv.at[zz, xs], {"seq": mate})
+
+    def kcopy():
+        return remote(sent, got, ksend, krecv, {"seq": s - 1})
+
+    greet = [(z > 0, {"dp": z - 1}), (z < n_z - 1, {"dp": z + 1}), (s >= 0, {"seq": mate})]
+    greet += [(s >= 0, {"seq": 2 * lax.rem(x + j, n_x) + c}) for j in range(1, n_x)]
+    greet += [((c == 0) & (s > 0), {"seq": s - 1}), ((c == 1) & (s < n_s - 1), {"seq": s + 1})]
+    barrier = pltpu.get_barrier_semaphore()
+    for there, target in greet:
+        @pl.when(there)
+        def _():
+            pl.semaphore_signal(barrier, inc=1, device_id=target,
+                                device_id_type=pl.DeviceIdType.MESH)
+    pl.semaphore_wait(barrier, sum(jnp.where(there, 1, 0) for there, _ in greet))
+
+    def hand_on(first):
+        if first:
+            rst_ref[...] = jnp.zeros_like(rst_ref)
+            sent[...] = local_ref[...].astype(BF16)
+            kcopy().start()
+        else:
+            kcopy().wait_recv()
+            rst_ref[...] = got[...]
+
+            @pl.when(s > 0)
+            def _():
+                joined = joined_ref[0:1, 0:1]
+                sent[...] = (local_ref[...] + got[...].astype(F32) * joined).astype(BF16)
+                kcopy().start()
+
+    def level(t):
+        if t == 0:
+            return ((z >= 0, z),)
+        return ((z - t >= 0, z - t), (z + t < n_z, z + t))
+
+    def spread(zz):
+        for j in range(1, n_x):
+            xs = lax.rem(x + j, n_x)
+            xland(zz, xs).wait_recv()
+            ccopy(zz, xs, buf.at[zz, 2 * xs + c]).start()
+
+    def add(zz):
+        for xs in range(n_x):
+            cland(zz, xs).wait_recv()
+
+        def one(sp, carry):
+            for at in range(0, width, span):
+                cols = slice(at, at + span)
+                wg_ref[:, cols] += mm(grads_ref[zz * n_s + sp], buf[zz, sp, :, cols], 1, 0)
+            return carry
+
+        lax.fori_loop(0, n_s, one, 0)
+
+    def over(t, act):
+        for there, zz in level(t):
+            @pl.when(there)
+            def _():
+                act(zz)
+
+    own = pltpu.make_async_copy(normed_ref, buf.at[z, s], own_sem)
+    own.start()
+
+    @pl.when(z < n_z - 1)
+    def _():
+        zcopy(True, z, normed_ref).start()
+
+    @pl.when(z > 0)
+    def _():
+        zcopy(False, z, normed_ref).start()
+
+    @pl.when(s == n_s - 1)
+    def _():
+        hand_on(True)
+
+    ccopy(z, x, normed_ref).start()
+
+    @pl.when((s >= n_s // 2) & (s < n_s - 1))
+    def _():
+        hand_on(False)
+
+    for j in range(1, n_x):
+        xcopy(z, j, normed_ref).start()
+    wg_ref[...] = jnp.zeros_like(wg_ref)
+    own.wait()
+
+    for t in range(1, n_z):
+        for up, (there, zz) in zip((True, False), level(t)):
+            @pl.when(there)
+            def _():
+                block = buf.at[zz, s]
+                zcopy(up, zz, block).wait_recv()
+
+                @pl.when((z < n_z - 1) if up else (z > 0))
+                def _():
+                    zcopy(up, zz, block).start()
+
+                ccopy(zz, x, block).start()
+                for j in range(1, n_x):
+                    xcopy(zz, j, block).start()
+        if t == 1:
+            @pl.when(s < n_s // 2)
+            def _():
+                hand_on(False)
+        over(t - 1, spread)
+        if t > 1:
+            over(t - 2, add)
+    over(n_z - 1, spread)
+    for t in range(max(n_z - 2, 0), n_z):
+        over(t, add)
+
+    def drain(zz):
+        for xs in range(n_x):
+            ccopy(zz, xs, normed_ref).wait_send()
+        for j in range(1, n_x):
+            xcopy(zz, j, normed_ref).wait_send()
+
+    for t in range(n_z):
+        over(t, drain)
+        for up, (there, zz) in zip((True, False), level(t) if t else ((z >= 0, z),) * 2):
+            @pl.when(there & ((z < n_z - 1) if up else (z > 0)))
+            def _():
+                zcopy(up, zz, normed_ref).wait_send()
+
+    @pl.when(s > 0)
+    def _():
+        kcopy().wait_send()
+
+
+def gather_grad(grads, normed, local_r, joined, n_z, n_s):
+    rows, width = normed.shape
+    n_x = n_s // 2
+    dma = pltpu.SemaphoreType.DMA
+    vmem = pl.BlockSpec(memory_space=pltpu.VMEM)
+    return pl.pallas_call(
+        functools.partial(gather_body, n_z, n_s),
+        out_shape=(
+            jax.ShapeDtypeStruct((grads.shape[1], width), F32),
+            jax.ShapeDtypeStruct((HS, width), BF16),
+        ),
+        in_specs=[vmem] * 4,
+        out_specs=[vmem] * 2,
+        scratch_shapes=[
+            pltpu.VMEM((n_z, n_s, rows, width), BF16),
+            pltpu.VMEM((HS, width), BF16),
+            pltpu.VMEM((HS, width), BF16),
+            dma((2, n_z)), dma((n_z,)),
+            dma((n_z, n_x)), dma((n_z, n_x)),
+            dma((n_z, n_x)), dma((n_z, n_x)),
+            dma, dma, dma,
+        ],
+        compiler_params=pltpu.CompilerParams(collective_id=0, has_side_effects=True),
+    )(grads, normed, local_r, joined)
+
+
+def neighbour(value, axis, step):
     peers, place = lax.axis_size(axis), lax.axis_index(axis)
-    step = -1 if reverse else 1
-    before = jnp.take(ids, jnp.clip(place - step, 0, peers - 1))
-    joined = before == jnp.take(ids, place)
+    pairs = [(i, i + step) for i in range(peers) if 0 <= i + step < peers]
+    got = lax.ppermute(jnp.broadcast_to(value, (1, HS)), axis, pairs)[0, 0]
+    return jnp.where(place == (0 if step == 1 else peers - 1), -1.0, got)
+
+
+def chain(local, joined, axis):
     got = jnp.zeros(local.shape, BF16)
-    for hop in range(peers - 1):
-        at = peers - 1 - hop if reverse else hop
+    for hop in range(lax.axis_size(axis) - 1):
         sent = local if hop == 0 else local + jnp.where(joined, got.astype(F32), 0.0)
-        got = got + lax.ppermute(sent.astype(BF16), axis, [(at, at + step)])
-    first = place == (peers - 1 if reverse else 0)
-    return got, jnp.where(first, jnp.full_like(before, -1.0), before)
+        got = got + lax.ppermute(sent.astype(BF16), axis, [(hop, hop + 1)])
+    return got
+
+
+def whole_rows(part, axis):
+    peers, place = lax.axis_size(axis), lax.axis_index(axis)
+    rows, cols = part.shape
+    full = jnp.zeros((rows, peers * cols), part.dtype)
+    full = lax.dynamic_update_slice(full, part, (0, place * cols))
+    for j in range(1, peers):
+        got = lax.ppermute(part, axis, [(i, (i + j) % peers) for i in range(peers)])
+        full = lax.dynamic_update_slice(full, got, (0, lax.rem(place + peers - j, peers) * cols))
+    return full
 
 
 def local(queries, key_rows, value_rows, row_plan, segments, norm_gain, out_weight, out_grad):
@@ -131,25 +333,27 @@
     pick_hot = (pick[:, None] == jnp.arange(slots_all, dtype=jnp.int32)[None, :]).astype(BF16)
 
     seg_f = segments[0].astype(F32)
-    edges = lax.all_gather(jnp.stack([seg_f[0], seg_f[-1]]), "seq")
+    id_in = neighbour(seg_f[-1], "seq", 1)
+    rid_in = neighbour(seg_f[0], "seq", -1)
     causal = positions[None, :] <= positions[:, None]
     same_doc = (causal & (seg_f[:, None] == seg_f[None, :])).astype(F32)
     tail = (seg_f == seg_f[-1]).astype(BF16)[:, None]
     head_part = (seg_f == seg_f[0]).astype(BF16)[:, None]
 
-    full_grad = lax.all_gather(out_grad, "mp", axis=1, tiled=True)
+    full_grad = whole_rows(out_grad, "mp")
     d_normed = lax.dot_general(
         full_grad, out_weight, (((1,), (1,)), ((), ())), preferred_element_type=F32
     )
     grad_cols = full_grad.T.reshape(devices, full_grad.shape[1] // devices, row_total)
     grad_cols = lax.all_to_all(grad_cols, ("dp", "seq"), split_axis=0, concat_axis=0, tiled=True)
+    grad_cols, d_normed = lax.optimization_barrier((grad_cols, d_normed))
 
     half = jax.ShapeDtypeStruct((row_total, width), BF16)
     state = jax.ShapeDtypeStruct((HS, width), F32)
     q, k, v, local_state = by_heads(
         place_body, heads, (pick_hot, tail), arrived, (half, half, half, state)
     )
-    state_in, id_in = chain(local_state, edges[:, 1], "seq", False)
+    state_in = chain(local_state, id_in == seg_f[-1], "seq")
     carried = (seg_f == id_in).astype(F32)[:, None]
     gain_row = norm_gain.reshape(1, width)
     normed, d_half, local_r = by_heads(
@@ -159,8 +363,10 @@
         (gain_row, q, k, v, state_in, d_normed),
         (half, half, state),
     )
-    everyone = lax.all_gather(normed, ("dp", "seq"), axis=0)
-    rstate_in, rid_in = chain(local_r, edges[:, 0], "seq", True)
+    rejoined = jnp.broadcast_to((rid_in == seg_f[0]).astype(F32), (8, HS))
+    weight_grad, rstate_in = gather_grad(
+        grad_cols, normed, local_r, rejoined, groups, lax.axis_size("seq")
+    )
     rev_use = (seg_f == rid_in).astype(F32)[:, None]
     dquery, dkey, dvalue = by_heads(
         backward_body,
@@ -168,9 +374,6 @@
         (same_doc, carried, rev_use),
         (q, k, v, d_half, state_in, rstate_in),
         (half, half, half),
-    )
-    weight_grad = lax.dot_general(
-        grad_cols, everyone, (((0, 2), (0, 1)), ((), ())), preferred_element_type=F32
     )
     return normed, dquery, dkey, dvalue, weight_grad
 

time: 223 us -> 192 us (0.86)
  Pallas kernels: 19.8 us -> 81.9 us
  waiting for transfers between devices: 80.3 us -> 35.9 us
  blocking collectives: 18.2 us -> 0 us
  between operations: 17.3 us -> 2.23 us
  other arithmetic: 21.7 us -> 12.7 us
  matrix products: 21.2 us -> 13.8 us
  local copies, waits for them, and re-layouts: 8.18 us -> 12.2 us
    pallas_call x0 -> x1, Pallas kernels: none -> 62 us  [gather_grad(): pl.pallas_call(functools.partial(gather_body, n_z, n_s), out_shape=(jax.S...]
    all_gather x1 -> x0, waiting for transfers between devices: 43.3 us -> none  [local(): everyone = lax.all_gather(normed, ('dp', 'seq'), axis=0)]
    all_gather x1 -> x0, blocking collectives: 12.2 us -> none  [local(): full_grad = lax.all_gather(out_grad, 'mp', axis=1, tiled=True)]
    all_to_all x3, waiting for transfers between devices: 16.7 us -> 27.9 us  [hand(): return lax.all_to_all(packed, 'dp', split_axis=0, concat_axis=0, tiled=True)]
    all_to_all x1, waiting for transfers between devices: 12.3 us -> 2.37 us  [local(): lax.all_to_all(grad_cols, ('dp', 'seq'), split_axis=0, concat_axis=0, til...]
    unnamed x1 -> x0, blocking collectives: 5.93 us -> none
    dot_general x1 -> x0, matrix products: 5.66 us -> none  [local(): lax.dot_general(grad_cols, everyone, (((0, 2), (0, 1)), ((), ())), prefer...]
    convert_element_type x6 -> x3, other arithmetic: 8.4 us -> 3.61 us  [chain(): got = got + lax.ppermute(sent.astype(BF16), axis, [(hop, hop + 1)])]
  transfers between devices with their start and end apart: 11 -> 10, of which waited for: 7 -> 5; matrix products, arithmetic and copies ran while one was open for 16% -> 16% of each run, Pallas kernels for 3% -> 0%
where the time goes in v2:
time: 192 us; the launch traced here: 191 us
  Pallas kernels  81.9 us (43%)
  waiting for transfers between devices  35.9 us (19%)
  starting transfers between devices  31.8 us (17%)
  matrix products  13.8 us (7%)
  other arithmetic  12.7 us (7%)
  local copies, waits for them, and re-layouts  12.2 us (6%)
  between operations  2.23 us (1%)
    pallas_call x1, Pallas kernels, gather_grad(): pl.pallas_call(functools.partial(gather_body, n_z, n_s), out_shape=(jax.S...  62 us
    all_to_all x3, waiting for transfers between devices, hand(): return lax.all_to_all(packed, 'dp', split_axis=0, concat_axis=0, tiled=True)  27.9 us
    pallas_call x3, Pallas kernels, by_heads(): pl.pallas_call(functools.partial(body, blocks), grid=(heads // blocks,),...  20 us
    all_to_all x3, starting transfers between devices, hand(): return lax.all_to_all(packed, 'dp', split_axis=0, concat_axis=0, tiled=True)  18.8 us
    dot_general x1, matrix products, local(): lax.dot_general(full_grad, out_weight, (((1,), (1,)), ((), ())), preferre...  10.1 us
    ppermute x1, waiting for transfers between devices, whole_rows(): got = lax.ppermute(part, axis, [(i, (i + j) % peers) for i in range(peers)])  5.69 us
    all_to_all x1, starting transfers between devices, local(): lax.all_to_all(grad_cols, ('dp', 'seq'), split_axis=0, concat_axis=0, til...  5.64 us
    ppermute x3, starting transfers between devices, chain(): got = got + lax.ppermute(sent.astype(BF16), axis, [(hop, hop + 1)])  4.26 us
  transfers between devices with their start and end apart: 10, of which 5 were waited for; matrix products, arithmetic and copies ran while one was open for 16% of the time, Pallas kernels for 0%

profile of v2, /device:TPU:12, one launch (start us, length us, event | category | flops | bytes accessed | tf_op | source)
XLA Modules:
  0.0 190.5 jit_solution(10196896702662291094)
XLA Ops:
  0.7 0.8 reduce_window_sum.22
  1.5 0.9 reduce_window_sum.23
  2.3 0.7 fusion.13
  3.2 1.2 convolution_convert_fusion.2
  4.4 5.3 %all-to-all-start = ((bf16[4,40,2048]{2,1,0:T(8,128)(2,1)}), bf16[4,40,2048]{2,1,0:T(8,128)(2,1)S(1)}, u32[]{:S(2)}, u32[]{:S(2)}) async-start(bf16[4,40,2048]{2,1,0:T(8,128)(2,1)} %bitcast.15), calls=%async_computation | async-start | bytes 1310720 | tf_op jit(solution)/shard_map/all_to_all | solution.py:326
  9.7 1.2 convolution_convert_fusion.1
  10.9 12.8 %all-to-all-done = bf16[4,40,2048]{2,1,0:T(8,128)(2,1)S(1)} async-done(((bf16[4,40,2048]{2,1,0:T(8,128)(2,1)}), bf16[4,40,2048]{2,1,0:T(8,128)(2,1)S(1)}, u32[]{:S(2)}, u32[]{:S(2)}) %all-to-all-start) | async-done | bytes 655392 | tf_op jit(solution)/shard_map/all_to_all | solution.py:326
  23.7 6.7 %all-to-all-start.1 = ((bf16[4,40,2048]{2,1,0:T(8,128)(2,1)}), bf16[4,40,2048]{2,1,0:T(8,128)(2,1)S(1)}, u32[]{:S(2)}, u32[]{:S(2)}) async-start(bf16[4,40,2048]{2,1,0:T(8,128)(2,1)} %bitcast.17), calls=%async_computation.1 | async-start | bytes 1310720 | tf_op jit(solution)/shard_map/all_to_all | solution.py:326
  30.5 1.2 convolution_convert_fusion
  31.7 12.4 %all-to-all-done.1 = bf16[4,40,2048]{2,1,0:T(8,128)(2,1)S(1)} async-done(((bf16[4,40,2048]{2,1,0:T(8,128)(2,1)}), bf16[4,40,2048]{2,1,0:T(8,128)(2,1)S(1)}, u32[]{:S(2)}, u32[]{:S(2)}) %all-to-all-start.1) | async-done | bytes 655392 | tf_op jit(solution)/shard_map/all_to_all | solution.py:326
  44.0 6.7 %all-to-all-start.2 = ((bf16[4,40,2048]{2,1,0:T(8,128)(2,1)}), bf16[4,40,2048]{2,1,0:T(8,128)(2,1)S(1)}, u32[]{:S(2)}, u32[]{:S(2)}) async-start(bf16[4,40,2048]{2,1,0:T(8,128)(2,1)} %bitcast.19), calls=%async_computation.2 | async-start | bytes 1310720 | tf_op jit(solution)/shard_map/all_to_all | solution.py:326
  50.8 0.6 fusion.15
  51.4 0.6 broadcast_in_dim.31
  52.0 1.3 collective-permute-start
  53.3 0.6 eq.111
  54.0 1.3 collective-permute-start.5
  55.5 0.7 fusion.14
  56.2 2.6 %fusion.9 = s32[128]{0:T(128)S(1)} fusion(s32[128]{0:T(128)S(1)} %convert_reduce_fusion, s32[]{:T(128)} %bitcast.8, s32[]{:T(128)} %bitcast.9, s32[]{:T(128)} %bitcast.11, s32[]{:T(128)} %bitcast.10), kind=kLoop, calls=%fused_computation.36 | loop fusion | flops 2432 | bytes 1040 | tf_op jit(solution)/shard_map/sub | solution.py:332
  58.8 0.7 fusion.pick_ref
  59.6 1.3 fusion.11
  60.9 0.7 copy.20.tail_ref
  61.7 2.7 %all-to-all-done.2 = bf16[4,40,2048]{2,1,0:T(8,128)(2,1)S(1)} async-done(((bf16[4,40,2048]{2,1,0:T(8,128)(2,1)}), bf16[4,40,2048]{2,1,0:T(8,128)(2,1)S(1)}, u32[]{:S(2)}, u32[]{:S(2)}) %all-to-all-start.2) | async-done | bytes 655392 | tf_op jit(solution)/shard_map/all_to_all | solution.py:326
  64.4 0.8 copy-done.5
  65.2 4.6 %shard_map.119 = (bf16[128,2048]{1,0:T(8,128)(2,1)}, bf16[128,2048]{1,0:T(8,128)(2,1)}, bf16[128,2048]{1,0:T(8,128)(2,1)}, f32[128,2048]{1,0:T(8,128)}) custom-call(bf16[128,160]{1,0:T(8,128)(2,1)} %fusion.pick_ref, bf16[128,1]{1,0:T(8,128)(2,1)} %copy.20.tail_ref, bf16[160,2048]{1,0:T(8,128)(2,1)} %bitcast.43, bf16[160,2048]{1,0:T(8,128)(2,1)} %bitcast.44, ...), custom_call_target="tpu_custom_call" | custom-call | flops 536870912 | bytes 4628736 | tf_op jit(solution)/shard_map/pallas_call | solution.py:79
  69.8 1.4 convert_element_type.133
  71.2 2.1 %collective-permute-start.1 = (bf16[128,2048]{1,0:T(8,128)(2,1)S(1)}, bf16[128,2048]{1,0:T(8,128)(2,1)S(1)}, u32[]{:S(2)}, u32[]{:S(2)}) collective-permute-start(bf16[128,2048]{1,0:T(8,128)(2,1)S(1)} %convert_element_type.133), channel_id=1, source_target_pairs={{0,2},{1,3},{8,10},{9,11},{16,18},{17,19},{24,26},{25,27}} | collective-permute-start | bytes 1572872 | tf_op jit(solution)/shard_map/ppermute | solution.py:292
  73.3 0.6 collective-permute-start.4
  74.9 1.5 collective-permute-start.2
  76.4 1.0 broadcast_in_dim.55
  77.4 0.8 constant_dynamic-update-slice_fusion.1
  78.1 5.7 %collective-permute-done.4 = bf16[128,1536]{1,0:T(8,128)(2,1)} collective-permute-done((bf16[128,1536]{1,0:T(8,128)(2,1)S(1)}, bf16[128,1536]{1,0:T(8,128)(2,1)}, u32[]{:S(2)}, u32[]{:S(2)}) %collective-permute-start.4) | collective-permute-done | bytes 393248 | tf_op jit(solution)/shard_map/ppermute | solution.py:302
  83.8 1.2 copy.22
  85.1 0.8 constant_dynamic-update-slice_fusion
  85.8 5.6 %all-to-all-start.3 = ((bf16[16,192,128]{2,1,0:T(8,128)(2,1)}), bf16[16,192,128]{2,1,0:T(8,128)(2,1)S(1)}, u32[]{:S(2)}, u32[]{:S(2)}) async-start(bf16[16,192,128]{2,1,0:T(8,128)(2,1)} %bitcast.22), calls=%async_computation.3 | async-start | bytes 1572864 | tf_op jit(solution)/shard_map/all_to_all | solution.py:348
  91.5 0.7 fusion.2.doc_ref
  92.9 0.7 copy.23.carried_ref
  93.6 0.7 copy.24.headp_ref
  94.3 0.7 copy.26.rev_ref
  95.1 2.1 %add_convert_fusion = (bf16[128,2048]{1,0:T(8,128)(2,1)}, bf16[128,2048]{1,0:T(8,128)(2,1)S(1)}) fusion(f32[128,2048]{1,0:T(8,128)S(1)} %copy-done.1, pred[]{:T(512)S(6)} %eq.120, bf16[128,2048]{1,0:T(8,128)(2,1)S(1)} %collective-permute-done.1, bf16[128,2048]{1,0:T(8,128)(2,1)} %collective-permute-done.2), kind=kLoop, calls=%fused_computation.3 | loop fusion | flops 1310720 | bytes 3145729 | tf_op jit(solution)/shard_map/convert_element_type | solution.py:292
  97.1 0.7 collective-permute-start.3
  97.8 10.1 %fusion.17.dn_ref = f32[128,2048]{1,0:T(8,128)} fusion(bf16[128,3072]{0,1:T(8,128)(2,1)} %constant_dynamic-update-slice_fusion, bf16[2048,3072]{1,0:T(8,128)(2,1)} %param.16), kind=kOutput, calls=%fused_computation.45 | convolution fusion | flops 1610612736 | bytes 14417920 | tf_op jit(solution)/shard_map/dot_general | solution.py:344
  108.0 2.4 %all-to-all-done.3.grads_ref = bf16[16,192,128]{2,1,0:T(8,128)(2,1)S(1)} async-done(((bf16[16,192,128]{2,1,0:T(8,128)(2,1)}), bf16[16,192,128]{2,1,0:T(8,128)(2,1)S(1)}, u32[]{:S(2)}, u32[]{:S(2)}) %all-to-all-start.3) | async-done | bytes 786464 | tf_op jit(solution)/shard_map/all_to_all | solution.py:348
  110.3 1.0 add.94.st_ref
  111.4 8.8 %shard_map.120 = (bf16[128,2048]{1,0:T(8,128)(2,1)}, bf16[128,2048]{1,0:T(8,128)(2,1)}, f32[128,2048]{1,0:T(8,128)}) custom-call(f32[128,128]{1,0:T(8,128)} %fusion.2.doc_ref, f32[128,1]{1,0:T(8,128)} %copy.23.carried_ref, bf16[128,1]{1,0:T(8,128)(2,1)} %copy.24.headp_ref, f32[1,2048]{1,0:T(1,128)} %bitcast.46, bf16[128,2048]{1,0:T(8,128)(2,1)} %get-tuple-element.20.q_ref, ...), custom_call_target="tpu_custom_call" | custom-call | flops 536870912 | bytes 5317376 | tf_op jit(solution)/shard_map/pallas_call | solution.py:79
  120.2 0.6 broadcast_in_dim.56.joined_ref
  120.8 62.0 %shard_map.121 = (f32[192,2048]{1,0:T(8,128)}, bf16[128,2048]{1,0:T(8,128)(2,1)}) custom-call(bf16[16,192,128]{2,1,0:T(8,128)(2,1)} %copy-done.2, bf16[128,2048]{1,0:T(8,128)(2,1)} %get-tuple-element.79.normed_ref, f32[128,2048]{1,0:T(8,128)} %get-tuple-element.28.local_ref, f32[8,128]{1,0:T(8,128)} %broadcast_in_dim.56.joined_ref), custom_call_target="tpu_custom_call" | custom-call | tf_op jit(solution)/shard_map/pallas_call | solution.py:260
  182.8 6.6 %shard_map.122 = (bf16[128,2048]{1,0:T(8,128)(2,1)}, bf16[128,2048]{1,0:T(8,128)(2,1)}, bf16[128,2048]{1,0:T(8,128)(2,1)}) custom-call(f32[128,128]{1,0:T(8,128)} %fusion.2.doc_ref, f32[128,1]{1,0:T(8,128)} %copy.23.carried_ref, f32[128,1]{1,0:T(8,128)} %copy.26.rev_ref, bf16[128,2048]{1,0:T(8,128)(2,1)} %get-tuple-element.20.q_ref, ...), custom_call_target="tpu_custom_call" | custom-call | flops 536870912 | bytes 4785152 | tf_op jit(solution)/shard_map/pallas_call | solution.py:79
  189.4 1.1 copy.30
  (37 shorter events, 0.9 us)
Async XLA Ops:
  0.6 2.5 %copy-start = (bf16[128,2048]{1,0:T(8,128)(2,1)S(1)}, bf16[128,2048]{1,0:T(8,128)(2,1)}, u32[]{:S(2)}) copy-start(bf16[128,2048]{1,0:T(8,128)(2,1)} %param.10) | copy-start | bytes 1572868
  0.6 9.1 %copy-start.7 = (bf16[128,2048]{1,0:T(8,128)(2,1)S(1)}, bf16[128,2048]{1,0:T(8,128)(2,1)}, u32[]{:S(2)}) copy-start(bf16[128,2048]{1,0:T(8,128)(2,1)} %param.11) | copy-start | bytes 1572868
  4.4 19.3 %all-to-all-start = ((bf16[4,40,2048]{2,1,0:T(8,128)(2,1)}), bf16[4,40,2048]{2,1,0:T(8,128)(2,1)S(1)}, u32[]{:S(2)}, u32[]{:S(2)}) async-start(bf16[4,40,2048]{2,1,0:T(8,128)(2,1)} %bitcast.15), calls=%async_computation | async-start | bytes 1310720 | tf_op jit(solution)/shard_map/all_to_all | solution.py:326
  9.7 20.8 %copy-start.11 = (s32[1,128]{1,0:T(1,128)S(1)}, s32[1,128]{1,0:T(1,128)}, u32[]{:S(2)}) copy-start(s32[1,128]{1,0:T(1,128)} %param.14) | copy-start | bytes 1540
  9.7 20.8 %copy-start.8 = (bf16[128,2048]{1,0:T(8,128)(2,1)S(1)}, bf16[128,2048]{1,0:T(8,128)(2,1)}, u32[]{:S(2)}) copy-start(bf16[128,2048]{1,0:T(8,128)(2,1)} %param.12) | copy-start | bytes 1572868
  23.7 20.3 %copy-start.3 = (bf16[4,40,2048]{2,1,0:T(8,128)(2,1)}, bf16[4,40,2048]{2,1,0:T(8,128)(2,1)S(1)}, u32[]{:S(2)}) copy-start(bf16[4,40,2048]{2,1,0:T(8,128)(2,1)S(1)} %all-to-all-done) | copy-start | bytes 1966084
  23.7 20.3 %all-to-all-start.1 = ((bf16[4,40,2048]{2,1,0:T(8,128)(2,1)}), bf16[4,40,2048]{2,1,0:T(8,128)(2,1)S(1)}, u32[]{:S(2)}, u32[]{:S(2)}) async-start(bf16[4,40,2048]{2,1,0:T(8,128)(2,1)} %bitcast.17), calls=%async_computation.1 | async-start | bytes 1310720 | tf_op jit(solution)/shard_map/all_to_all | solution.py:326
  30.5 24.8 %copy-start.10 = (s32[4,4]{1,0:T(4,128)S(1)}, s32[4,4]{1,0:T(4,128)}, u32[]{:S(2)}) copy-start(s32[4,4]{1,0:T(4,128)} %param.13) | copy-start | bytes 196
  44.0 20.3 %copy-start.4 = (bf16[4,40,2048]{2,1,0:T(8,128)(2,1)}, bf16[4,40,2048]{2,1,0:T(8,128)(2,1)S(1)}, u32[]{:S(2)}) copy-start(bf16[4,40,2048]{2,1,0:T(8,128)(2,1)S(1)} %all-to-all-done.1) | copy-start | bytes 1966084
  44.0 20.3 %all-to-all-start.2 = ((bf16[4,40,2048]{2,1,0:T(8,128)(2,1)}), bf16[4,40,2048]{2,1,0:T(8,128)(2,1)S(1)}, u32[]{:S(2)}, u32[]{:S(2)}) async-start(bf16[4,40,2048]{2,1,0:T(8,128)(2,1)} %bitcast.19), calls=%async_computation.2 | async-start | bytes 1310720 | tf_op jit(solution)/shard_map/all_to_all | solution.py:326
  52.0 7.5 %collective-permute-start = (f32[1,128]{1,0:T(1,128)S(1)}, f32[1,128]{1,0:T(1,128)S(1)}, u32[]{:S(2)}, u32[]{:S(2)}) collective-permute-start(f32[1,128]{1,0:T(1,128)S(1)} %broadcast_in_dim.31), channel_id=1, source_target_pairs={{0,2},{2,4},{4,6},{1,3},{3,5},{5,7},{8,10},{10,12},{12,14},{9,11},... | collective-permute-start | bytes 1544 | tf_op jit(solution)/shard_map/ppermute | solution.py:284
  54.0 5.6 %collective-permute-start.5 = (f32[1,128]{1,0:T(1,128)S(1)}, f32[1,128]{1,0:T(1,128)S(1)}, u32[]{:S(2)}, u32[]{:S(2)}) collective-permute-start(f32[1,128]{1,0:T(1,128)S(1)} %eq.111), channel_id=1, source_target_pairs={{2,0},{4,2},{6,4},{3,1},{5,3},{7,5},{10,8},{12,10},{14,12},{11,9},... | collective-permute-start | bytes 1544 | tf_op jit(solution)/shard_map/ppermute | solution.py:284
  64.4 0.8 copy-start.5
  69.8 3.5 %copy-start.9 = (bf16[128,1536]{1,0:T(8,128)(2,1)S(1)}, bf16[128,1536]{1,0:T(8,128)(2,1)}, u32[]{:S(2)}) copy-start(bf16[128,1536]{1,0:T(8,128)(2,1)} %param.17) | copy-start | bytes 1179652
  69.8 5.0 %copy-start.1 = (f32[128,2048]{1,0:T(8,128)S(1)}, f32[128,2048]{1,0:T(8,128)}, u32[]{:S(2)}) copy-start(f32[128,2048]{1,0:T(8,128)} %get-tuple-element.23) | copy-start | bytes 3145732
  71.2 3.6 %collective-permute-start.1 = (bf16[128,2048]{1,0:T(8,128)(2,1)S(1)}, bf16[128,2048]{1,0:T(8,128)(2,1)S(1)}, u32[]{:S(2)}, u32[]{:S(2)}) collective-permute-start(bf16[128,2048]{1,0:T(8,128)(2,1)S(1)} %convert_element_type.133), channel_id=1, source_target_pairs={{0,2},{1,3},{8,10},{9,11},{16,18},{17,19},{24,26},{25,27}} | collective-permute-start | bytes 1572872 | tf_op jit(solution)/shard_map/ppermute | solution.py:292
  73.3 10.5 %collective-permute-start.4 = (bf16[128,1536]{1,0:T(8,128)(2,1)S(1)}, bf16[128,1536]{1,0:T(8,128)(2,1)}, u32[]{:S(2)}, u32[]{:S(2)}) collective-permute-start(bf16[128,1536]{1,0:T(8,128)(2,1)S(1)} %copy-done.9), channel_id=1, source_target_pairs={{0,1},{1,0},{2,3},{3,2},{4,5},{5,4},{6,7},{7,6},{8,9},{9,8},{10,11... | collective-permute-start | bytes 1179656 | tf_op jit(solution)/shard_map/ppermute | solution.py:302
  74.9 20.1 %collective-permute-start.2 = (bf16[128,2048]{1,0:T(8,128)(2,1)S(1)}, bf16[128,2048]{1,0:T(8,128)(2,1)}, u32[]{:S(2)}, u32[]{:S(2)}) collective-permute-start(bf16[128,2048]{1,0:T(8,128)(2,1)S(1)} %add_convert_fusion.1), channel_id=1, source_target_pairs={{2,4},{3,5},{10,12},{11,13},{18,20},{19,21},{26,28},{27,29}} | collective-permute-start | bytes 1572872 | tf_op jit(solution)/shard_map/ppermute | solution.py:292
  85.8 24.5 %all-to-all-start.3 = ((bf16[16,192,128]{2,1,0:T(8,128)(2,1)}), bf16[16,192,128]{2,1,0:T(8,128)(2,1)S(1)}, u32[]{:S(2)}, u32[]{:S(2)}) async-start(bf16[16,192,128]{2,1,0:T(8,128)(2,1)} %bitcast.22), calls=%async_computation.3 | async-start | bytes 1572864 | tf_op jit(solution)/shard_map/all_to_all | solution.py:348
  97.1 13.2 %collective-permute-start.3 = (bf16[128,2048]{1,0:T(8,128)(2,1)}, bf16[128,2048]{1,0:T(8,128)(2,1)S(1)}, u32[]{:S(2)}, u32[]{:S(2)}) collective-permute-start(bf16[128,2048]{1,0:T(8,128)(2,1)} %get-tuple-element.56), channel_id=1, source_target_pairs={{4,6},{5,7},{12,14},{13,15},{20,22},{21,23},{28,30},{29,31}} | collective-permute-start | bytes 1572872 | tf_op jit(solution)/shard_map/ppermute | solution.py:292
  110.3 9.8 %copy-start.2 = (bf16[16,192,128]{2,1,0:T(8,128)(2,1)}, bf16[16,192,128]{2,1,0:T(8,128)(2,1)S(1)}, u32[]{:S(2)}) copy-start(bf16[16,192,128]{2,1,0:T(8,128)(2,1)S(1)} %all-to-all-done.3.grads_ref) | copy-start | bytes 2359300
  182.8 6.6 %copy-start.6 = (f32[192,2048]{1,0:T(8,128)S(1)}, f32[192,2048]{1,0:T(8,128)}, u32[]{:S(2)}) copy-start(f32[192,2048]{1,0:T(8,128)} %get-tuple-element.83) | copy-start | bytes 4718596

commit v3 on v2

--- a/solution.py
+++ b/solution.py
@@ -19,14 +19,117 @@
     return lax.dot_general(a, b, (((ca,), (cb,)), ((), ())), preferred_element_type=F32)
 
 
-def place_body(blocks, pick_ref, tail_ref, aq_ref, ak_ref, av_ref, q_ref, k_ref, v_ref, st_ref):
-    pick = pick_ref[...]
+def exchange_body(
+    n_z, n_m, shot_ref, pick_ref, tail_ref, qi_ref, ki_ref, vi_ref, og_ref, w_ref,
+    q_ref, k_ref, v_ref, st_ref, dn_ref, full_ref,
+    packed, landed, weight, parts, ssem, rsem, msend, mrecv, wsem,
+):
+    z, m = lax.axis_index("dp"), lax.axis_index("mp")
+    width = qi_ref.shape[1]
+    span = 512 if width % 512 == 0 else HS
+    fetch = pltpu.make_async_copy(w_ref, weight, wsem)
+    fetch.start()
+    barrier = pltpu.get_barrier_semaphore()
+    peers = [{"mp": lax.rem(m + j, n_m)} for j in range(1, n_m)]
+    peers += [{"dp": lax.rem(z + j, n_z)} for j in range(1, n_z)]
+    for target in peers:
+        pl.semaphore_signal(barrier, inc=1, device_id=target,
+                            device_id_type=pl.DeviceIdType.MESH)
+    pl.semaphore_wait(barrier, len(peers))
+
+    def mcopy(j, source):
+        return pltpu.make_async_remote_copy(
+            src_ref=og_ref, dst_ref=parts.at[source], send_sem=msend.at[j],
+            recv_sem=mrecv.at[source], device_id={"mp": lax.rem(m + j, n_m)},
+            device_id_type=pl.DeviceIdType.MESH,
+        )
+
+    def zcopy(a, j, source):
+        return pltpu.make_async_remote_copy(
+            src_ref=packed.at[a, lax.rem(z + j, n_z)], dst_ref=landed.at[a, source],
+            send_sem=ssem.at[a, j], recv_sem=rsem.at[a, source],
+            device_id={"dp": lax.rem(z + j, n_z)}, device_id_type=pl.DeviceIdType.MESH,
+        )
+
+    for j in range(1, n_m):
+        mcopy(j, m).start()
+    ins = (ki_ref, vi_ref, qi_ref)
+    outs = (k_ref, v_ref, q_ref)
+    for a in range(3):
+        for j in range(n_z):
+            for at in range(0, width, span):
+                cols = slice(at, at + span)
+                packed[a, j, :, cols] = mm(shot_ref[j], ins[a][:, cols], 1, 0).astype(BF16)
+        if a:
+            for j in range(1, n_z):
+                zcopy(a - 1, j, z).start()
+    parts[m] = og_ref[...]
+    for a in range(3):
+        landed[a, z] = packed[a, z]
+    for j in range(1, n_z):
+        zcopy(2, j, z).start()
+
+    for j in range(1, n_m):
+        mcopy(j, lax.rem(m + j, n_m)).wait_recv()
+    full_ref[...] = parts[...]
+    fetch.wait()
+    part = og_ref.shape[1]
+
+    def block(i, carry):
+        total = mm(parts[0], weight[i, :, 0:part], 1, 1)
+        for j in range(1, n_m):
+            total += mm(parts[j], weight[i, :, j * part:(j + 1) * part], 1, 1)
+        dn_ref[:, pl.ds(pl.multiple_of(i * HS, HS), HS)] = total
+        return carry
+
+    lax.fori_loop(0, width // HS, block, 0)
     tail = tail_ref[...]
-    for src, dst in ((aq_ref, q_ref), (ak_ref, k_ref), (av_ref, v_ref)):
-        dst[...] = mm(pick, src[...], 1, 0).astype(BF16)
-    for h in range(blocks):
-        cols = slice(h * HS, (h + 1) * HS)
-        st_ref[:, cols] = mm(k_ref[:, cols] * tail, v_ref[:, cols], 0, 0)
+    for a in range(3):
+        for j in range(1, n_z):
+            zcopy(a, j, lax.rem(z + j, n_z)).wait_recv()
+        for at in range(0, width, span):
+            cols = slice(at, at + span)
+            rows = mm(pick_ref[0], landed[a, 0, :, cols], 1, 0)
+            for j in range(1, n_z):
+                rows += mm(pick_ref[j], landed[a, j, :, cols], 1, 0)
+            outs[a][:, cols] = rows.astype(BF16)
+        if a == 1:
+            for at in range(0, width, HS):
+                cols = slice(at, at + HS)
+                st_ref[:, cols] = mm(k_ref[:, cols] * tail, v_ref[:, cols], 0, 0)
+    for j in range(1, n_m):
+        mcopy(j, m).wait_send()
+    for a in range(3):
+        for j in range(1, n_z):
+            zcopy(a, j, z).wait_send()
+
+
+def exchange(send_hot, pick_hot, tail, queries, key_rows, value_rows, out_grad, weight, n_z, n_m):
+    rows, width = queries.shape
+    cap = send_hot.shape[1]
+    dma = pltpu.SemaphoreType.DMA
+    vmem = pl.BlockSpec(memory_space=pltpu.VMEM)
+    half = jax.ShapeDtypeStruct((rows, width), BF16)
+    weight = weight.reshape(width // HS, HS, weight.shape[1])
+    return pl.pallas_call(
+        functools.partial(exchange_body, n_z, n_m),
+        out_shape=(
+            half, half, half,
+            jax.ShapeDtypeStruct((HS, width), F32),
+            jax.ShapeDtypeStruct((rows, width), F32),
+            jax.ShapeDtypeStruct((n_m, *out_grad.shape), BF16),
+        ),
+        in_specs=[vmem] * 7 + [pl.BlockSpec(memory_space=pl.ANY)],
+        out_specs=[vmem] * 6,
+        scratch_shapes=[
+            pltpu.VMEM((3, n_z, cap, width), BF16),
+            pltpu.VMEM((3, n_z, cap, width), BF16),
+            pltpu.VMEM(weight.shape, BF16),
+            pltpu.VMEM((n_m, *out_grad.shape), BF16),
+            dma((3, n_z)), dma((3, n_z)), dma((n_m,)), dma((n_m,)), dma,
+        ],
+        compiler_params=pltpu.CompilerParams(collective_id=1, has_side_effects=True),
+    )(send_hot, pick_hot, tail, queries, key_rows, value_rows, out_grad, weight)
 
 
 def forward_body(
@@ -293,17 +396,6 @@
     return got
 
 
-def whole_rows(part, axis):
-    peers, place = lax.axis_size(axis), lax.axis_index(axis)
-    rows, cols = part.shape
-    full = jnp.zeros((rows, peers * cols), part.dtype)
-    full = lax.dynamic_update_slice(full, part, (0, place * cols))
-    for j in range(1, peers):
-        got = lax.ppermute(part, axis, [(i, (i + j) % peers) for i in range(peers)])
-        full = lax.dynamic_update_slice(full, got, (0, lax.rem(place + peers - j, peers) * cols))
-    return full
-
-
 def local(queries, key_rows, value_rows, row_plan, segments, norm_gain, out_weight, out_grad):
     row_total = queries.shape[0]
     width = queries.shape[1]
@@ -320,17 +412,13 @@
     my_send = jnp.take(send_start, my_group, axis=0)
     send_index = jnp.minimum(my_send[:, None] + slots[None, :], row_total - 1).reshape(-1)
     send_hot = (send_index[:, None] == positions[None, :]).astype(BF16)
-
-    def hand(x):
-        packed = jnp.dot(send_hot, x, preferred_element_type=F32).astype(BF16)
-        return lax.all_to_all(packed, "dp", split_axis=0, concat_axis=0, tiled=True)
-
-    arrived = (hand(queries), hand(key_rows), hand(value_rows))
+    send_hot = send_hot.reshape(groups, capacity, row_total)
     my_start = jnp.take(recv_start, my_group, axis=1)
     my_end = my_start + jnp.take(row_plan, my_group, axis=1)
     source = jnp.sum((my_end[None, :] <= positions[:, None]).astype(jnp.int32), axis=1)
     pick = source * capacity + positions - jnp.take(my_start, source)
-    pick_hot = (pick[:, None] == jnp.arange(slots_all, dtype=jnp.int32)[None, :]).astype(BF16)
+    all_slots = jnp.arange(slots_all, dtype=jnp.int32).reshape(groups, 1, capacity)
+    pick_hot = (pick[None, :, None] == all_slots).astype(BF16)
 
     seg_f = segments[0].astype(F32)
     id_in = neighbour(seg_f[-1], "seq", 1)
@@ -340,19 +428,15 @@
     tail = (seg_f == seg_f[-1]).astype(BF16)[:, None]
     head_part = (seg_f == seg_f[0]).astype(BF16)[:, None]
 
-    full_grad = whole_rows(out_grad, "mp")
-    d_normed = lax.dot_general(
-        full_grad, out_weight, (((1,), (1,)), ((), ())), preferred_element_type=F32
-    )
-    grad_cols = full_grad.T.reshape(devices, full_grad.shape[1] // devices, row_total)
+    q, k, v, local_state, d_normed, full_grad = exchange(
+        send_hot, pick_hot, tail, queries, key_rows, value_rows, out_grad, out_weight,
+        groups, lax.axis_size("mp"),
+    )
+    grad_cols = full_grad.transpose(0, 2, 1).reshape(devices, -1, row_total)
     grad_cols = lax.all_to_all(grad_cols, ("dp", "seq"), split_axis=0, concat_axis=0, tiled=True)
-    grad_cols, d_normed = lax.optimization_barrier((grad_cols, d_normed))
 
     half = jax.ShapeDtypeStruct((row_total, width), BF16)
     state = jax.ShapeDtypeStruct((HS, width), F32)
-    q, k, v, local_state = by_heads(
-        place_body, heads, (pick_hot, tail), arrived, (half, half, half, state)
-    )
     state_in = chain(local_state, id_in == seg_f[-1], "seq")
     carried = (seg_f == id_in).astype(F32)[:, None]
     gain_row = norm_gain.reshape(1, width)

time: 192 us -> 173 us (0.901)
  Pallas kernels: 81.9 us -> 129 us
  waiting for transfers between devices: 35.9 us -> 4.42 us
  starting transfers between devices: 31.8 us -> 13.1 us
  matrix products: 13.8 us -> 0 us
  local copies, waits for them, and re-layouts: 12.2 us -> 8.65 us
    pallas_call x0 -> x1, Pallas kernels: none -> 52 us  [exchange(): pl.pallas_call(functools.partial(exchange_body, n_z, n_m), out_shape=(hal...]
    all_to_all x3 -> x0, waiting for transfers between devices: 27.9 us -> none  [hand(): return lax.all_to_all(packed, 'dp', split_axis=0, concat_axis=0, tiled=True)]
    all_to_all x3 -> x0, starting transfers between devices: 18.8 us -> none  [hand(): return lax.all_to_all(packed, 'dp', split_axis=0, concat_axis=0, tiled=True)]
    dot_general x4 -> x0, matrix products: 13.8 us -> none  [the longest x1 10.1 us: local(): lax.dot_general(full_grad, out_weight, (((1,), (1,)), ((), ())), preferre...]
    ppermute x1 -> x0, waiting for transfers between devices: 5.69 us -> none  [whole_rows(): got = lax.ppermute(part, axis, [(i, (i + j) % peers) for i in range(peers)])]
    pallas_call x3 -> x2, Pallas kernels: 20 us -> 15.4 us  [by_heads(): pl.pallas_call(functools.partial(body, blocks), grid=(heads // blocks,),...]
  transfers between devices with their start and end apart: 10 -> 6, of which waited for: 5 -> 2; matrix products, arithmetic and copies ran while one was open for 16% -> 9% of each run, Pallas kernels for 0% -> 5%
where the time goes in v3:
time: 173 us; the launch traced here: 172 us
  Pallas kernels  129 us (75%)
  other arithmetic  14.3 us (8%)
  starting transfers between devices  13.1 us (8%)
  local copies, waits for them, and re-layouts  8.65 us (5%)
  waiting for transfers between devices  4.42 us (3%)
  between operations  2.16 us (1%)
    pallas_call x1, Pallas kernels, gather_grad(): pl.pallas_call(functools.partial(gather_body, n_z, n_s), out_shape=(jax.S...  61.9 us
    pallas_call x1, Pallas kernels, exchange(): pl.pallas_call(functools.partial(exchange_body, n_z, n_m), out_shape=(hal...  52 us
    pallas_call x2, Pallas kernels, by_heads(): pl.pallas_call(functools.partial(body, blocks), grid=(heads // blocks,),...  15.4 us
    all_to_all x1, starting transfers between devices, local(): lax.all_to_all(grad_cols, ('dp', 'seq'), split_axis=0, concat_axis=0, til...  5.8 us
    ppermute x3, starting transfers between devices, chain(): got = got + lax.ppermute(sent.astype(BF16), axis, [(hop, hop + 1)])  4.22 us
    all_to_all x1, waiting for transfers between devices, local(): lax.all_to_all(grad_cols, ('dp', 'seq'), split_axis=0, concat_axis=0, til...  3.58 us
  transfers between devices with their start and end apart: 6, of which 2 were waited for; matrix products, arithmetic and copies ran while one was open for 9% of the time, Pallas kernels for 5%

profile of v3, /device:TPU:12, one launch (start us, length us, event | category | flops | bytes accessed | tf_op | source)
XLA Modules:
  0.0 171.9 jit_solution(15295213220852792308)
XLA Ops:
  0.6 0.7 fusion.13
  1.3 0.6 fusion.12
  1.9 0.6 broadcast_in_dim.29
  2.5 1.7 %collective-permute-start = (f32[1,128]{1,0:T(1,128)S(1)}, f32[1,128]{1,0:T(1,128)S(1)}, u32[]{:S(2)}, u32[]{:S(2)}) collective-permute-start(f32[1,128]{1,0:T(1,128)S(1)} %broadcast_in_dim.29), channel_id=1, source_target_pairs={{0,2},{2,4},{4,6},{1,3},{3,5},{5,7},{8,10},{10,12},{12,14},{9,11},... | collective-permute-start | bytes 1544 | tf_op jit(solution)/shard_map/ppermute | solution.py:387
  4.3 0.6 eq.112
  4.9 1.3 collective-permute-start.4
  6.2 0.9 reduce_window_sum.22
  7.1 0.7 reduce_window_sum.23
  7.8 0.7 fusion.10
  8.5 0.9 select_reduce_fusion
  9.4 0.6 fusion.11
  10.0 0.1 convert_reduce_fusion
  10.1 0.1 add_minimum_fusion
  10.2 2.5 %fusion.6 = s32[128]{0:T(128)S(1)} fusion(s32[128]{0:T(128)S(1)} %convert_reduce_fusion, s32[]{:T(128)} %bitcast.9, s32[]{:T(128)} %bitcast.10, s32[]{:T(128)} %bitcast.12, s32[]{:T(128)} %bitcast.11), kind=kLoop, calls=%fused_computation.29 | loop fusion | flops 2432 | bytes 1040 | tf_op jit(solution)/shard_map/sub | solution.py:419
  12.7 0.8 compare_convert_fusion.pick_ref
  13.4 0.7 fusion.shot_ref
  14.1 0.0 collective-permute-done
  14.2 0.0 collective-permute-done.4
  14.2 2.0 %fusion.8 = (f32[128,1]{0,1:T(1,128)S(1)}, f32[128,1]{0,1:T(1,128)S(1)}, bf16[128,1]{0,1:T(2,128)(2,1)S(1)}, bf16[128,1]{0,1:T(2,128)(2,1)S(1)}) fusion(f32[]{:T(128)S(6)} %select_n.75, s32[1,128]{1,0:T(1,128)} %param.14, f32[]{:T(128)S(6)} %select_n.66, f32[]{:T(128)} %bitcast.4, f32[]{:T(128)} %bitcast.1), kind=kLoop, calls=%fused_computation.31 | loop fusion | flops 1152 | bytes 2064 | tf_op jit(solution)/shard_map/convert_element_type | solution.py:454
  16.2 0.7 copy.19.tail_ref
  16.9 52.0 %shard_map.119 = (bf16[128,2048]{1,0:T(8,128)(2,1)}, bf16[128,2048]{1,0:T(8,128)(2,1)}, bf16[128,2048]{1,0:T(8,128)(2,1)}, f32[128,2048]{1,0:T(8,128)}, f32[128,...) custom-call(bf16[4,40,128]{2,1,0:T(8,128)(2,1)} %fusion.shot_ref, bf16[4,128,40]{2,1,0:T(8,128)(2,1)} %compare_convert_fusion.pick_ref, ...), custom_call_target="tpu_custom_call" | custom-call | tf_op jit(solution)/shard_map/pallas_call | solution.py:114
  69.0 0.0 copy-start
  69.0 0.0 copy-start.3
  69.0 1.4 convert_element_type.125
  70.4 2.1 %collective-permute-start.1 = (bf16[128,2048]{1,0:T(8,128)(2,1)S(1)}, bf16[128,2048]{1,0:T(8,128)(2,1)S(1)}, u32[]{:S(2)}, u32[]{:S(2)}) collective-permute-start(bf16[128,2048]{1,0:T(8,128)(2,1)S(1)} %convert_element_type.125), channel_id=1, source_target_pairs={{0,2},{1,3},{8,10},{9,11},{16,18},{17,19},{24,26},{25,27}} | collective-permute-start | bytes 1572872 | tf_op jit(solution)/shard_map/ppermute | solution.py:395
  73.1 0.8 collective-permute-done.1
  74.0 0.0 copy-done
  74.0 0.1 add_convert_fusion.1
  74.1 1.5 collective-permute-start.2
  75.6 0.0 copy-done.3
  75.6 1.2 copy.22
  76.8 5.8 %all-to-all-start = ((bf16[16,192,128]{2,1,0:T(8,128)(2,1)}), bf16[16,192,128]{2,1,0:T(8,128)(2,1)S(1)}, u32[]{:S(2)}, u32[]{:S(2)}) async-start(bf16[16,192,128]{2,1,0:T(8,128)(2,1)} %bitcast.19), calls=%async_computation | async-start | bytes 1572864 | tf_op jit(solution)/shard_map/all_to_all | solution.py:436
  82.6 0.0 collective-permute-done.2
  82.6 1.3 add_convert_fusion
  83.9 0.7 collective-permute-start.3
  84.6 0.7 fusion.2.doc_ref
  85.9 0.7 copy.20.carried_ref
  86.7 0.7 copy.21.headp_ref
  87.4 0.7 copy.24.rev_ref
  88.1 0.0 collective-permute-done.3
  88.1 0.9 add.93.st_ref
  89.0 8.8 %shard_map.120 = (bf16[128,2048]{1,0:T(8,128)(2,1)}, bf16[128,2048]{1,0:T(8,128)(2,1)}, f32[128,2048]{1,0:T(8,128)}) custom-call(f32[128,128]{1,0:T(8,128)} %fusion.2.doc_ref, f32[128,1]{1,0:T(8,128)} %copy.20.carried_ref, bf16[128,1]{1,0:T(8,128)(2,1)} %copy.21.headp_ref, f32[1,2048]{1,0:T(1,128)} %bitcast.34, bf16[128,2048]{1,0:T(8,128)(2,1)} %get-tuple-element.20.q_ref, ...), custom_call_target="tpu_custom_call" | custom-call | flops 536870912 | bytes 5317376 | tf_op jit(solution)/shard_map/pallas_call | solution.py:182
  97.8 3.6 %all-to-all-done.grads_ref = bf16[16,192,128]{2,1,0:T(8,128)(2,1)S(1)} async-done(((bf16[16,192,128]{2,1,0:T(8,128)(2,1)}), bf16[16,192,128]{2,1,0:T(8,128)(2,1)S(1)}, u32[]{:S(2)}, u32[]{:S(2)}) %all-to-all-start) | async-done | bytes 786464 | tf_op jit(solution)/shard_map/all_to_all | solution.py:436
  101.4 0.6 broadcast_in_dim.51.joined_ref
  102.0 0.3 copy-done.1
  102.3 61.9 %shard_map.121 = (f32[192,2048]{1,0:T(8,128)}, bf16[128,2048]{1,0:T(8,128)(2,1)}) custom-call(bf16[16,192,128]{2,1,0:T(8,128)(2,1)} %copy-done.1, bf16[128,2048]{1,0:T(8,128)(2,1)} %get-tuple-element.79.normed_ref, f32[128,2048]{1,0:T(8,128)} %get-tuple-element.28.local_ref, f32[8,128]{1,0:T(8,128)} %broadcast_in_dim.51.joined_ref), custom_call_target="tpu_custom_call" | custom-call | tf_op jit(solution)/shard_map/pallas_call | solution.py:363
  164.2 6.6 %shard_map.122 = (bf16[128,2048]{1,0:T(8,128)(2,1)}, bf16[128,2048]{1,0:T(8,128)(2,1)}, bf16[128,2048]{1,0:T(8,128)(2,1)}) custom-call(f32[128,128]{1,0:T(8,128)} %fusion.2.doc_ref, f32[128,1]{1,0:T(8,128)} %copy.20.carried_ref, f32[128,1]{1,0:T(8,128)} %copy.24.rev_ref, bf16[128,2048]{1,0:T(8,128)(2,1)} %get-tuple-element.20.q_ref, ...), custom_call_target="tpu_custom_call" | custom-call | flops 536870912 | bytes 4785152 | tf_op jit(solution)/shard_map/pallas_call | solution.py:182
  170.8 1.1 copy.26
  (6 shorter events, 0.0 us)
Async XLA Ops:
  2.5 11.6 %collective-permute-start = (f32[1,128]{1,0:T(1,128)S(1)}, f32[1,128]{1,0:T(1,128)S(1)}, u32[]{:S(2)}, u32[]{:S(2)}) collective-permute-start(f32[1,128]{1,0:T(1,128)S(1)} %broadcast_in_dim.29), channel_id=1, source_target_pairs={{0,2},{2,4},{4,6},{1,3},{3,5},{5,7},{8,10},{10,12},{12,14},{9,11},... | collective-permute-start | bytes 1544 | tf_op jit(solution)/shard_map/ppermute | solution.py:387
  4.9 9.3 %collective-permute-start.4 = (f32[1,128]{1,0:T(1,128)S(1)}, f32[1,128]{1,0:T(1,128)S(1)}, u32[]{:S(2)}, u32[]{:S(2)}) collective-permute-start(f32[1,128]{1,0:T(1,128)S(1)} %eq.112), channel_id=1, source_target_pairs={{2,0},{4,2},{6,4},{3,1},{5,3},{7,5},{10,8},{12,10},{14,12},{11,9},... | collective-permute-start | bytes 1544 | tf_op jit(solution)/shard_map/ppermute | solution.py:387
  69.0 5.0 %copy-start = (f32[128,2048]{1,0:T(8,128)S(1)}, f32[128,2048]{1,0:T(8,128)}, u32[]{:S(2)}) copy-start(f32[128,2048]{1,0:T(8,128)} %get-tuple-element.23) | copy-start | bytes 3145732
  69.0 6.6 %copy-start.3 = (bf16[2,128,1536]{2,1,0:T(8,128)(2,1)S(1)}, bf16[2,128,1536]{2,1,0:T(8,128)(2,1)}, u32[]{:S(2)}) copy-start(bf16[2,128,1536]{2,1,0:T(8,128)(2,1)} %get-tuple-element.27) | copy-start | bytes 2359300
  70.4 3.6 %collective-permute-start.1 = (bf16[128,2048]{1,0:T(8,128)(2,1)S(1)}, bf16[128,2048]{1,0:T(8,128)(2,1)S(1)}, u32[]{:S(2)}, u32[]{:S(2)}) collective-permute-start(bf16[128,2048]{1,0:T(8,128)(2,1)S(1)} %convert_element_type.125), channel_id=1, source_target_pairs={{0,2},{1,3},{8,10},{9,11},{16,18},{17,19},{24,26},{25,27}} | collective-permute-start | bytes 1572872 | tf_op jit(solution)/shard_map/ppermute | solution.py:395
  74.1 8.5 %collective-permute-start.2 = (bf16[128,2048]{1,0:T(8,128)(2,1)S(1)}, bf16[128,2048]{1,0:T(8,128)(2,1)}, u32[]{:S(2)}, u32[]{:S(2)}) collective-permute-start(bf16[128,2048]{1,0:T(8,128)(2,1)S(1)} %add_convert_fusion.1), channel_id=1, source_target_pairs={{2,4},{3,5},{10,12},{11,13},{18,20},{19,21},{26,28},{27,29}} | collective-permute-start | bytes 1572872 | tf_op jit(solution)/shard_map/ppermute | solution.py:395
  76.8 24.6 %all-to-all-start = ((bf16[16,192,128]{2,1,0:T(8,128)(2,1)}), bf16[16,192,128]{2,1,0:T(8,128)(2,1)S(1)}, u32[]{:S(2)}, u32[]{:S(2)}) async-start(bf16[16,192,128]{2,1,0:T(8,128)(2,1)} %bitcast.19), calls=%async_computation | async-start | bytes 1572864 | tf_op jit(solution)/shard_map/all_to_all | solution.py:436
  83.9 4.3 %collective-permute-start.3 = (bf16[128,2048]{1,0:T(8,128)(2,1)S(1)}, bf16[128,2048]{1,0:T(8,128)(2,1)S(1)}, u32[]{:S(2)}, u32[]{:S(2)}) collective-permute-start(bf16[128,2048]{1,0:T(8,128)(2,1)S(1)} %get-tuple-element.56), channel_id=1, source_target_pairs={{4,6},{5,7},{12,14},{13,15},{20,22},{21,23},{28,30},{29,31}} | collective-permute-start | bytes 1572872 | tf_op jit(solution)/shard_map/ppermute | solution.py:395
  101.4 0.9 copy-start.1
  164.2 6.6 %copy-start.2 = (f32[192,2048]{1,0:T(8,128)S(1)}, f32[192,2048]{1,0:T(8,128)}, u32[]{:S(2)}) copy-start(f32[192,2048]{1,0:T(8,128)} %get-tuple-element.83) | copy-start | bytes 4718596

commit v4 on v3

--- a/solution.py
+++ b/solution.py
@@ -155,22 +155,13 @@
         r_ref[:, cols] = mm(q * headp, d_half, 0, 0)
 
 
-def backward_body(
-    blocks, doc_ref, carried_ref, rev_ref, q_ref, k_ref, v_ref, d_ref, st_ref, rst_ref,
-    dq_ref, dk_ref, dv_ref,
-):
-    doc = doc_ref[...]
-    carried = carried_ref[...]
-    rev = rev_ref[...]
-    for h in range(blocks):
-        cols = slice(h * HS, (h + 1) * HS)
-        q, k, v, d = q_ref[:, cols], k_ref[:, cols], v_ref[:, cols], d_ref[:, cols]
-        st, rst = st_ref[:, cols], rst_ref[:, cols]
-        p = (mm(q, k, 1, 1) * doc).astype(BF16)
-        dp = (mm(d, v, 1, 1) * doc).astype(BF16)
-        dq_ref[:, cols] = (mm(dp, k, 1, 0) + mm(d, st, 1, 1) * carried).astype(BF16)
-        dk_ref[:, cols] = (mm(dp, q, 0, 0) + mm(v, rst, 1, 1) * rev).astype(BF16)
-        dv_ref[:, cols] = (mm(p, d, 0, 0) + mm(k, rst, 1, 0) * rev).astype(BF16)
+def backward_head(cols, doc, carried, rev, refs, dq_ref, dk_ref, dv_ref):
+    q, k, v, d, st, rst = (ref[:, cols] for ref in refs)
+    p = (mm(q, k, 1, 1) * doc).astype(BF16)
+    dp = (mm(d, v, 1, 1) * doc).astype(BF16)
+    dq_ref[:, cols] = (mm(dp, k, 1, 0) + mm(d, st, 1, 1) * carried).astype(BF16)
+    dk_ref[:, cols] = (mm(dp, q, 0, 0) + mm(v, rst, 1, 1) * rev).astype(BF16)
+    dv_ref[:, cols] = (mm(p, d, 0, 0) + mm(k, rst, 1, 0) * rev).astype(BF16)
 
 
 def by_heads(body, heads, fixed, moving, outs):
@@ -192,8 +183,9 @@
 
 
 def gather_body(
-    n_z, n_s, grads_ref, normed_ref, local_ref, joined_ref, wg_ref, rst_ref,
-    buf, got, sent, zsend, zrecv, xsend, xrecv, csend, crecv, ksend, krecv, own_sem,
+    n_z, n_s, grads_ref, normed_ref, local_ref, joined_ref,
+    doc_ref, carried_ref, rev_ref, q_ref, k_ref, v_ref, d_ref, st_ref,
+    wg_ref, dq_ref, dk_ref, dv_ref, rst_ref, buf, got, sent, zsend, zrecv, xsend, xrecv, csend, crecv, ksend, krecv, own_sem,
 ):
     n_x = n_s // 2
     z, s = lax.axis_index("dp"), lax.axis_index("seq")
@@ -333,6 +325,16 @@
         over(t - 1, spread)
         if t > 1:
             over(t - 2, add)
+    def heads_at(i, carry):
+        doc, carried, rev = doc_ref[...], carried_ref[...], rev_ref[...]
+        for h in range(blocks):
+            cols = pl.ds(pl.multiple_of((i * blocks + h) * HS, HS), HS)
+            backward_head(cols, doc, carried, rev, (q_ref, k_ref, v_ref, d_ref, st_ref, rst_ref),
+                          dq_ref, dk_ref, dv_ref)
+        return carry
+
+    blocks = 4 if width % (4 * HS) == 0 else 1
+    lax.fori_loop(0, width // (blocks * HS), heads_at, 0)
     over(n_z - 1, spread)
     for t in range(max(n_z - 2, 0), n_z):
         over(t, add)
@@ -355,7 +357,7 @@
         kcopy().wait_send()
 
 
-def gather_grad(grads, normed, local_r, joined, n_z, n_s):
+def gather_grad(grads, normed, local_r, joined, others, n_z, n_s):
     rows, width = normed.shape
     n_x = n_s // 2
     dma = pltpu.SemaphoreType.DMA
@@ -364,11 +366,12 @@
         functools.partial(gather_body, n_z, n_s),
         out_shape=(
             jax.ShapeDtypeStruct((grads.shape[1], width), F32),
-            jax.ShapeDtypeStruct((HS, width), BF16),
+            *[jax.ShapeDtypeStruct((rows, width), BF16)] * 3,
         ),
-        in_specs=[vmem] * 4,
-        out_specs=[vmem] * 2,
+        in_specs=[vmem] * (4 + len(others)),
+        out_specs=[vmem] * 4,
         scratch_shapes=[
+            pltpu.VMEM((HS, width), BF16),
             pltpu.VMEM((n_z, n_s, rows, width), BF16),
             pltpu.VMEM((HS, width), BF16),
             pltpu.VMEM((HS, width), BF16),
@@ -378,7 +381,7 @@
             dma, dma, dma,
         ],
         compiler_params=pltpu.CompilerParams(collective_id=0, has_side_effects=True),
-    )(grads, normed, local_r, joined)
+    )(grads, normed, local_r, joined, *others)
 
 
 def neighbour(value, axis, step):
@@ -404,21 +407,19 @@
     my_group = lax.axis_index("dp")
     devices = groups * lax.axis_size("seq")
     capacity = row_total // min(groups, 8) + row_total // 16
-    slots_all = groups * capacity
-    send_start = jnp.cumsum(row_plan, axis=1) - row_plan
-    recv_start = jnp.cumsum(row_plan, axis=0) - row_plan
+    groups_at = jnp.arange(groups, dtype=jnp.int32)
+    below = (groups_at[:, None] < groups_at[None, :]).astype(jnp.int32)
+    mine = (groups_at == my_group).astype(jnp.int32)
+    to_others = jnp.sum(row_plan * mine[:, None], axis=0)
+    to_me = jnp.sum(row_plan * mine[None, :], axis=1)
+    my_send = jnp.sum(to_others[:, None] * below, axis=0)
+    my_start = jnp.sum(to_me[:, None] * below, axis=0)
     slots = jnp.arange(capacity, dtype=jnp.int32)
     positions = jnp.arange(row_total, dtype=jnp.int32)
-    my_send = jnp.take(send_start, my_group, axis=0)
-    send_index = jnp.minimum(my_send[:, None] + slots[None, :], row_total - 1).reshape(-1)
-    send_hot = (send_index[:, None] == positions[None, :]).astype(BF16)
-    send_hot = send_hot.reshape(groups, capacity, row_total)
-    my_start = jnp.take(recv_start, my_group, axis=1)
-    my_end = my_start + jnp.take(row_plan, my_group, axis=1)
-    source = jnp.sum((my_end[None, :] <= positions[:, None]).astype(jnp.int32), axis=1)
-    pick = source * capacity + positions - jnp.take(my_start, source)
-    all_slots = jnp.arange(slots_all, dtype=jnp.int32).reshape(groups, 1, capacity)
-    pick_hot = (pick[None, :, None] == all_slots).astype(BF16)
+    send_index = jnp.minimum(my_send[:, None] + slots[None, :], row_total - 1)
+    send_hot = (send_index[:, :, None] == positions[None, None, :]).astype(BF16)
+    placed = positions[None, :, None] - my_start[:, None, None] == slots[None, None, :]
+    pick_hot = (placed & (slots[None, None, :] < to_me[:, None, None])).astype(BF16)
 
     seg_f = segments[0].astype(F32)
     id_in = neighbour(seg_f[-1], "seq", 1)
@@ -448,16 +449,10 @@
         (half, half, state),
     )
     rejoined = jnp.broadcast_to((rid_in == seg_f[0]).astype(F32), (8, HS))
-    weight_grad, rstate_in = gather_grad(
-        grad_cols, normed, local_r, rejoined, groups, lax.axis_size("seq")
-    )
     rev_use = (seg_f == rid_in).astype(F32)[:, None]
-    dquery, dkey, dvalue = by_heads(
-        backward_body,
-        heads,
-        (same_doc, carried, rev_use),
-        (q, k, v, d_half, state_in, rstate_in),
-        (half, half, half),
+    others = (same_doc, carried, rev_use, q, k, v, d_half, state_in)
+    weight_grad, dquery, dkey, dvalue = gather_grad(
+        grad_cols, normed, local_r, rejoined, others, groups, lax.axis_size("seq")
     )
     return normed, dquery, dkey, dvalue, weight_grad
 

time: 173 us -> 171 us (0.988)
  other arithmetic: 14.3 us -> 9.77 us
  local copies, waits for them, and re-layouts: 8.65 us -> 12.7 us
    pallas_call x2 -> x1, Pallas kernels: 15.4 us -> 8.75 us  [by_heads(): pl.pallas_call(functools.partial(body, blocks), grid=(heads // blocks,),...]
    pallas_call x1, Pallas kernels: 61.9 us -> 67.4 us  [gather_grad(): pl.pallas_call(functools.partial(gather_body, n_z, n_s), out_shape=(jax.S...]
    unnamed x9 -> x14, local copies, waits for them, and re-layouts: 1.42 us -> 6.11 us
    sub x2 -> x1, other arithmetic: 3.19 us -> 0.07 us  [local(): positions[None, :, None] - my_start[:, None, None] == slots[None, None, :]]
  transfers between devices with their start and end apart: 6 -> 6, of which waited for: 2 -> 3; matrix products, arithmetic and copies ran while one was open for 9% -> 6% of each run, Pallas kernels for 5% -> 5%
where the time goes in v4:
time: 171 us; the launch traced here: 170 us
  Pallas kernels  128 us (75%)
  starting transfers between devices  12.8 us (7%)
  local copies, waits for them, and re-layouts  12.7 us (7%)
  other arithmetic  9.77 us (6%)
  waiting for transfers between devices  4.7 us (3%)
  between operations  2.17 us (1%)
    pallas_call x1, Pallas kernels, gather_grad(): pl.pallas_call(functools.partial(gather_body, n_z, n_s), out_shape=(jax.S...  67.4 us
    pallas_call x1, Pallas kernels, exchange(): pl.pallas_call(functools.partial(exchange_body, n_z, n_m), out_shape=(hal...  52 us
    pallas_call x1, Pallas kernels, by_heads(): pl.pallas_call(functools.partial(body, blocks), grid=(heads // blocks,),...  8.75 us
    unnamed x14, local copies, waits for them, and re-layouts  6.11 us
    all_to_all x1, starting transfers between devices, local(): lax.all_to_all(grad_cols, ('dp', 'seq'), split_axis=0, concat_axis=0, til...  5.5 us
    ppermute x3, starting transfers between devices, chain(): got = got + lax.ppermute(sent.astype(BF16), axis, [(hop, hop + 1)])  4.22 us
    all_to_all x1, waiting for transfers between devices, local(): lax.all_to_all(grad_cols, ('dp', 'seq'), split_axis=0, concat_axis=0, til...  3.57 us
  transfers between devices with their start and end apart: 6, of which 3 were waited for; matrix products, arithmetic and copies ran while one was open for 6% of the time, Pallas kernels for 5%

profile of v4, /device:TPU:12, one launch (start us, length us, event | category | flops | bytes accessed | tf_op | source)
XLA Modules:
  0.0 170.3 jit_solution(13104434687439005312)
XLA Ops:
  0.6 0.7 fusion.10
  1.3 0.6 fusion.9
  1.9 0.6 broadcast_in_dim.8
  2.5 1.7 %collective-permute-start = (f32[1,128]{1,0:T(1,128)S(1)}, f32[1,128]{1,0:T(1,128)S(1)}, u32[]{:S(2)}, u32[]{:S(2)}) collective-permute-start(f32[1,128]{1,0:T(1,128)S(1)} %broadcast_in_dim.8), channel_id=1, source_target_pairs={{0,2},{2,4},{4,6},{1,3},{3,5},{5,7},{8,10},{10,12},{12,14},{9,11},... | collective-permute-start | bytes 1544 | tf_op jit(solution)/shard_map/ppermute | solution.py:390
  4.3 0.6 eq.125
  4.9 1.3 collective-permute-start.4
  6.2 0.9 multiply_reduce_fusion
  7.1 0.1 iota_compare_fusion.3
  7.2 0.1 select_reduce_fusion
  7.3 0.1 iota_subtract_fusion
  7.4 0.1 add_minimum_fusion
  7.4 0.8 fusion.1.pick_ref
  8.2 0.7 fusion.2.shot_ref
  8.9 0.0 collective-permute-done
  9.0 0.3 collective-permute-done.4
  9.3 2.0 %fusion.8 = (f32[128,1]{0,1:T(1,128)S(1)}, f32[128,1]{0,1:T(1,128)S(1)}, bf16[128,1]{0,1:T(2,128)(2,1)S(1)}, bf16[128,1]{0,1:T(2,128)(2,1)S(1)}) fusion(f32[]{:T(128)S(6)} %select_n.23, s32[1,128]{1,0:T(1,128)} %param.12, f32[]{:T(128)S(6)} %select_n.19, f32[]{:T(128)} %bitcast.4, f32[]{:T(128)} %bitcast.1), kind=kLoop, calls=%fused_computation.26 | loop fusion | flops 1152 | bytes 2064 | tf_op jit(solution)/shard_map/convert_element_type | solution.py:452
  11.3 0.7 copy.19.tail_ref
  12.0 52.0 %shard_map.119 = (bf16[128,2048]{1,0:T(8,128)(2,1)}, bf16[128,2048]{1,0:T(8,128)(2,1)}, bf16[128,2048]{1,0:T(8,128)(2,1)}, f32[128,2048]{1,0:T(8,128)}, f32[128,...) custom-call(bf16[4,40,128]{2,1,0:T(8,128)(2,1)} %fusion.2.shot_ref, bf16[4,128,40]{2,1,0:T(8,128)(2,1)} %fusion.1.pick_ref, ...), custom_call_target="tpu_custom_call" | custom-call | tf_op jit(solution)/shard_map/pallas_call | solution.py:114
  64.0 0.0 copy-start
  64.0 0.0 copy-start.3
  64.0 1.4 convert_element_type.133
  65.5 2.1 %collective-permute-start.1 = (bf16[128,2048]{1,0:T(8,128)(2,1)S(1)}, bf16[128,2048]{1,0:T(8,128)(2,1)S(1)}, u32[]{:S(2)}, u32[]{:S(2)}) collective-permute-start(bf16[128,2048]{1,0:T(8,128)(2,1)S(1)} %convert_element_type.133), channel_id=1, source_target_pairs={{0,2},{1,3},{8,10},{9,11},{16,18},{17,19},{24,26},{25,27}} | collective-permute-start | bytes 1572872 | tf_op jit(solution)/shard_map/ppermute | solution.py:398
  68.2 0.8 collective-permute-done.1
  69.0 0.0 copy-done
  69.0 0.1 add_convert_fusion.1
  69.1 1.5 collective-permute-start.2
  70.6 0.0 copy-done.3
  70.6 1.2 copy.22
  71.8 5.5 %all-to-all-start = ((bf16[16,192,128]{2,1,0:T(8,128)(2,1)}), bf16[16,192,128]{2,1,0:T(8,128)(2,1)S(1)}, u32[]{:S(2)}, u32[]{:S(2)}) async-start(bf16[16,192,128]{2,1,0:T(8,128)(2,1)} %bitcast.10), calls=%async_computation | async-start | bytes 1572864 | tf_op jit(solution)/shard_map/all_to_all | solution.py:437
  77.3 0.0 collective-permute-done.2
  77.3 1.3 add_convert_fusion
  78.6 0.7 collective-permute-start.3
  79.3 0.7 fusion.4.doc_ref
  80.7 0.7 copy.21.headp_ref
  81.4 0.7 copy.24.rev_ref
  82.2 0.7 copy.20.carried_ref
  82.9 0.0 collective-permute-done.3
  82.9 0.9 add.35.st_ref
  83.8 8.8 %shard_map.120 = (bf16[128,2048]{1,0:T(8,128)(2,1)}, bf16[128,2048]{1,0:T(8,128)(2,1)}, f32[128,2048]{1,0:T(8,128)}) custom-call(f32[128,128]{1,0:T(8,128)} %fusion.4.doc_ref, f32[128,1]{1,0:T(8,128)} %copy.20.carried_ref, bf16[128,1]{1,0:T(8,128)(2,1)} %copy.21.headp_ref, f32[1,2048]{1,0:T(1,128)} %bitcast.22, bf16[128,2048]{1,0:T(8,128)(2,1)} %get-tuple-element.18.q_ref, ...), custom_call_target="tpu_custom_call" | custom-call | flops 536870912 | bytes 5317376 | tf_op jit(solution)/shard_map/pallas_call | solution.py:173
  92.6 3.6 %all-to-all-done.grads_ref = bf16[16,192,128]{2,1,0:T(8,128)(2,1)S(1)} async-done(((bf16[16,192,128]{2,1,0:T(8,128)(2,1)}), bf16[16,192,128]{2,1,0:T(8,128)(2,1)S(1)}, u32[]{:S(2)}, u32[]{:S(2)}) %all-to-all-start) | async-done | bytes 786464 | tf_op jit(solution)/shard_map/all_to_all | solution.py:437
  96.1 0.6 broadcast_in_dim.10.joined_ref
  96.8 0.3 copy-done.1
  97.0 67.4 %shard_map.121 = (f32[192,2048]{1,0:T(8,128)}, bf16[128,2048]{1,0:T(8,128)(2,1)}, bf16[128,2048]{1,0:T(8,128)(2,1)}, bf16[128,2048]{1,0:T(8,128)(2,1)}) custom-call(bf16[16,192,128]{2,1,0:T(8,128)(2,1)} %copy-done.1, bf16[128,2048]{1,0:T(8,128)(2,1)} %get-tuple-element.50.normed_ref, f32[128,2048]{1,0:T(8,128)} %get-tuple-element.25.local_ref, ...), custom_call_target="tpu_custom_call" | custom-call | tf_op jit(solution)/shard_map/pallas_call | solution.py:365
  164.4 2.0 %copy.29 = bf16[128,2048]{1,0:T(8,128)(2,1)} copy(bf16[128,2048]{1,0:T(8,128)(2,1)} %get-tuple-element.51) | data formatting | bytes 1048576
  166.5 1.9 %copy.30 = bf16[128,2048]{1,0:T(8,128)(2,1)} copy(bf16[128,2048]{1,0:T(8,128)(2,1)} %get-tuple-element.52) | data formatting | bytes 1048576
  168.3 0.8 copy.31
  169.1 0.0 copy-done.2
  169.1 1.1 copy.32
  (5 shorter events, 0.0 us)
Async XLA Ops:
  2.5 6.4 %collective-permute-start = (f32[1,128]{1,0:T(1,128)S(1)}, f32[1,128]{1,0:T(1,128)S(1)}, u32[]{:S(2)}, u32[]{:S(2)}) collective-permute-start(f32[1,128]{1,0:T(1,128)S(1)} %broadcast_in_dim.8), channel_id=1, source_target_pairs={{0,2},{2,4},{4,6},{1,3},{3,5},{5,7},{8,10},{10,12},{12,14},{9,11},... | collective-permute-start | bytes 1544 | tf_op jit(solution)/shard_map/ppermute | solution.py:390
  4.9 4.3 %collective-permute-start.4 = (f32[1,128]{1,0:T(1,128)S(1)}, f32[1,128]{1,0:T(1,128)S(1)}, u32[]{:S(2)}, u32[]{:S(2)}) collective-permute-start(f32[1,128]{1,0:T(1,128)S(1)} %eq.125), channel_id=1, source_target_pairs={{2,0},{4,2},{6,4},{3,1},{5,3},{7,5},{10,8},{12,10},{14,12},{11,9},... | collective-permute-start | bytes 1544 | tf_op jit(solution)/shard_map/ppermute | solution.py:390
  64.0 5.0 %copy-start = (f32[128,2048]{1,0:T(8,128)S(1)}, f32[128,2048]{1,0:T(8,128)}, u32[]{:S(2)}) copy-start(f32[128,2048]{1,0:T(8,128)} %get-tuple-element.21) | copy-start | bytes 3145732
  64.0 6.6 %copy-start.3 = (bf16[2,128,1536]{2,1,0:T(8,128)(2,1)S(1)}, bf16[2,128,1536]{2,1,0:T(8,128)(2,1)}, u32[]{:S(2)}) copy-start(bf16[2,128,1536]{2,1,0:T(8,128)(2,1)} %get-tuple-element.24) | copy-start | bytes 2359300
  65.5 3.5 %collective-permute-start.1 = (bf16[128,2048]{1,0:T(8,128)(2,1)S(1)}, bf16[128,2048]{1,0:T(8,128)(2,1)S(1)}, u32[]{:S(2)}, u32[]{:S(2)}) collective-permute-start(bf16[128,2048]{1,0:T(8,128)(2,1)S(1)} %convert_element_type.133), channel_id=1, source_target_pairs={{0,2},{1,3},{8,10},{9,11},{16,18},{17,19},{24,26},{25,27}} | collective-permute-start | bytes 1572872 | tf_op jit(solution)/shard_map/ppermute | solution.py:398
  69.1 8.2 %collective-permute-start.2 = (bf16[128,2048]{1,0:T(8,128)(2,1)S(1)}, bf16[128,2048]{1,0:T(8,128)(2,1)}, u32[]{:S(2)}, u32[]{:S(2)}) collective-permute-start(bf16[128,2048]{1,0:T(8,128)(2,1)S(1)} %add_convert_fusion.1), channel_id=1, source_target_pairs={{2,4},{3,5},{10,12},{11,13},{18,20},{19,21},{26,28},{27,29}} | collective-permute-start | bytes 1572872 | tf_op jit(solution)/shard_map/ppermute | solution.py:398
  71.8 24.3 %all-to-all-start = ((bf16[16,192,128]{2,1,0:T(8,128)(2,1)}), bf16[16,192,128]{2,1,0:T(8,128)(2,1)S(1)}, u32[]{:S(2)}, u32[]{:S(2)}) async-start(bf16[16,192,128]{2,1,0:T(8,128)(2,1)} %bitcast.10), calls=%async_computation | async-start | bytes 1572864 | tf_op jit(solution)/shard_map/all_to_all | solution.py:437
  78.6 4.3 %collective-permute-start.3 = (bf16[128,2048]{1,0:T(8,128)(2,1)S(1)}, bf16[128,2048]{1,0:T(8,128)(2,1)S(1)}, u32[]{:S(2)}, u32[]{:S(2)}) collective-permute-start(bf16[128,2048]{1,0:T(8,128)(2,1)S(1)} %get-tuple-element.33), channel_id=1, source_target_pairs={{4,6},{5,7},{12,14},{13,15},{20,22},{21,23},{28,30},{29,31}} | collective-permute-start | bytes 1572872 | tf_op jit(solution)/shard_map/ppermute | solution.py:398
  96.1 0.9 copy-start.1
  164.4 3.9 %copy-start.4 = (bf16[128,2048]{1,0:T(8,128)(2,1)S(1)}, bf16[128,2048]{1,0:T(8,128)(2,1)}, u32[]{:S(2)}) copy-start(bf16[128,2048]{1,0:T(8,128)(2,1)} %get-tuple-element.53) | copy-start | bytes 1572868
  164.4 4.7 %copy-start.2 = (f32[192,2048]{1,0:T(8,128)S(1)}, f32[192,2048]{1,0:T(8,128)}, u32[]{:S(2)}) copy-start(f32[192,2048]{1,0:T(8,128)} %get-tuple-element.54) | copy-start | bytes 4718596

commit v5 on v4

--- a/solution.py
+++ b/solution.py
@@ -422,8 +422,6 @@
     pick_hot = (placed & (slots[None, None, :] < to_me[:, None, None])).astype(BF16)
 
     seg_f = segments[0].astype(F32)
-    id_in = neighbour(seg_f[-1], "seq", 1)
-    rid_in = neighbour(seg_f[0], "seq", -1)
     causal = positions[None, :] <= positions[:, None]
     same_doc = (causal & (seg_f[:, None] == seg_f[None, :])).astype(F32)
     tail = (seg_f == seg_f[-1]).astype(BF16)[:, None]
@@ -438,6 +436,9 @@
 
     half = jax.ShapeDtypeStruct((row_total, width), BF16)
     state = jax.ShapeDtypeStruct((HS, width), F32)
+    edges, local_state = lax.optimization_barrier((seg_f, local_state))
+    id_in = neighbour(edges[-1], "seq", 1)
+    rid_in = neighbour(edges[0], "seq", -1)
     state_in = chain(local_state, id_in == seg_f[-1], "seq")
     carried = (seg_f == id_in).astype(F32)[:, None]
     gain_row = norm_gain.reshape(1, width)

time: 171 us -> 173 us (1.012)
  starting transfers between devices: 12.8 us -> 15.8 us
  waiting for transfers between devices: 4.7 us -> 1.84 us
    all_to_all x1, starting transfers between devices: 5.5 us -> 9.12 us  [local(): lax.all_to_all(grad_cols, ('dp', 'seq'), split_axis=0, concat_axis=0, til...]
    all_to_all x1, waiting for transfers between devices: 3.57 us -> 0.01 us  [local(): lax.all_to_all(grad_cols, ('dp', 'seq'), split_axis=0, concat_axis=0, til...]
    pallas_call x1, Pallas kernels: 67.4 us -> 69.6 us  [gather_grad(): pl.pallas_call(functools.partial(gather_body, n_z, n_s), out_shape=(jax.S...]
    unnamed x14 -> x16, local copies, waits for them, and re-layouts: 6.11 us -> 6.08 us
  transfers between devices with their start and end apart: 6 -> 6, of which waited for: 3 -> 2; matrix products, arithmetic and copies ran while one was open for 6% -> 5% of each run, Pallas kernels for 5% -> 5%
where the time goes in v5:
time: 173 us; the launch traced here: 172 us
  Pallas kernels  129 us (75%)
  starting transfers between devices  15.8 us (9%)
  local copies, waits for them, and re-layouts  13.3 us (8%)
  other arithmetic  9.76 us (6%)
  between operations  2.22 us (1%)
  waiting for transfers between devices  1.84 us (1%)
    pallas_call x1, Pallas kernels, gather_grad(): pl.pallas_call(functools.partial(gather_body, n_z, n_s), out_shape=(jax.S...  69.6 us
    pallas_call x1, Pallas kernels, exchange(): pl.pallas_call(functools.partial(exchange_body, n_z, n_m), out_shape=(hal...  51 us
    all_to_all x1, starting transfers between devices, local(): lax.all_to_all(grad_cols, ('dp', 'seq'), split_axis=0, concat_axis=0, til...  9.12 us
    pallas_call x1, Pallas kernels, by_heads(): pl.pallas_call(functools.partial(body, blocks), grid=(heads // blocks,),...  8.75 us
    unnamed x16, local copies, waits for them, and re-layouts  6.08 us
    ppermute x3, starting transfers between devices, chain(): got = got + lax.ppermute(sent.astype(BF16), axis, [(hop, hop + 1)])  4.11 us
  transfers between devices with their start and end apart: 6, of which 2 were waited for; matrix products, arithmetic and copies ran while one was open for 5% of the time, Pallas kernels for 5%

profile of v5, /device:TPU:12, one launch (start us, length us, event | category | flops | bytes accessed | tf_op | source)
XLA Modules:
  0.0 172.3 jit_solution(9075145791575874065)
XLA Ops:
  0.6 0.9 multiply_reduce_fusion
  1.5 0.1 iota_compare_fusion.3
  1.6 0.1 select_reduce_fusion
  1.7 0.7 fusion.11
  2.3 0.6 fusion.10
  2.9 1.3 fusion.5
  4.2 0.1 iota_subtract_fusion
  4.3 0.1 add_minimum_fusion
  4.4 0.7 copy.19.tail_ref
  5.1 0.7 fusion.2.shot_ref
  5.8 0.8 fusion.1.pick_ref
  6.6 51.0 %shard_map.119 = (bf16[128,2048]{1,0:T(8,128)(2,1)}, bf16[128,2048]{1,0:T(8,128)(2,1)}, bf16[128,2048]{1,0:T(8,128)(2,1)}, f32[128,2048]{1,0:T(8,128)}, f32[128,...) custom-call(bf16[4,40,128]{2,1,0:T(8,128)(2,1)} %fusion.2.shot_ref, bf16[4,128,40]{2,1,0:T(8,128)(2,1)} %fusion.1.pick_ref, ...), custom_call_target="tpu_custom_call" | custom-call | tf_op jit(solution)/shard_map/pallas_call | solution.py:114
  57.6 0.0 copy-start
  57.6 0.0 copy-start.3
  57.6 1.4 convert_element_type.133
  59.0 1.9 %collective-permute-start.1 = (bf16[128,2048]{1,0:T(8,128)(2,1)S(1)}, bf16[128,2048]{1,0:T(8,128)(2,1)S(1)}, u32[]{:S(2)}, u32[]{:S(2)}) collective-permute-start(bf16[128,2048]{1,0:T(8,128)(2,1)S(1)} %convert_element_type.133), channel_id=1, source_target_pairs={{0,2},{1,3},{8,10},{9,11},{16,18},{17,19},{24,26},{25,27}} | collective-permute-start | bytes 1572872 | tf_op jit(solution)/shard_map/ppermute | solution.py:398
  61.0 0.6 fusion.9
  61.6 0.6 broadcast_in_dim.10
  62.2 1.3 collective-permute-start
  63.5 0.8 collective-permute-done
  65.0 0.0 collective-permute-done.1
  65.0 0.1 add_convert_fusion.1
  65.2 1.5 collective-permute-start.2
  66.7 1.2 copy.22
  67.9 9.1 %all-to-all-start = ((bf16[16,192,128]{2,1,0:T(8,128)(2,1)}), bf16[16,192,128]{2,1,0:T(8,128)(2,1)S(1)}, u32[]{:S(2)}, u32[]{:S(2)}) async-start(bf16[16,192,128]{2,1,0:T(8,128)(2,1)} %bitcast.11), calls=%async_computation | async-start | bytes 1572864 | tf_op jit(solution)/shard_map/all_to_all | solution.py:435
  77.0 0.0 collective-permute-done.2
  77.0 1.3 add_convert_fusion
  78.3 0.7 collective-permute-start.3
  79.0 0.6 broadcast_in_dim.12
  79.6 1.3 collective-permute-start.4
  80.9 0.7 fusion.4.doc_ref
  81.7 1.0 collective-permute-done.4
  83.4 0.7 fusion.8
  84.1 0.7 copy.21.headp_ref
  84.8 0.7 copy.24.rev_ref
  85.5 0.7 copy.20.carried_ref
  86.2 0.0 collective-permute-done.3
  86.2 0.9 add.35.st_ref
  87.2 8.8 %shard_map.120 = (bf16[128,2048]{1,0:T(8,128)(2,1)}, bf16[128,2048]{1,0:T(8,128)(2,1)}, f32[128,2048]{1,0:T(8,128)}) custom-call(f32[128,128]{1,0:T(8,128)} %fusion.4.doc_ref, f32[128,1]{1,0:T(8,128)} %copy.20.carried_ref, bf16[128,1]{1,0:T(8,128)(2,1)} %copy.21.headp_ref, f32[1,2048]{1,0:T(1,128)} %bitcast.24, bf16[128,2048]{1,0:T(8,128)(2,1)} %get-tuple-element.22.q_ref, ...), custom_call_target="tpu_custom_call" | custom-call | flops 536870912 | bytes 5317376 | tf_op jit(solution)/shard_map/pallas_call | solution.py:173
  95.9 0.0 all-to-all-done.grads_ref
  95.9 0.0 copy-start.1
  95.9 0.6 broadcast_in_dim.13.joined_ref
  96.6 0.2 copy-done.1
  96.8 69.6 %shard_map.121 = (f32[192,2048]{1,0:T(8,128)}, bf16[128,2048]{1,0:T(8,128)(2,1)}, bf16[128,2048]{1,0:T(8,128)(2,1)}, bf16[128,2048]{1,0:T(8,128)(2,1)}) custom-call(bf16[16,192,128]{2,1,0:T(8,128)(2,1)} %copy-done.1, bf16[128,2048]{1,0:T(8,128)(2,1)} %get-tuple-element.55.normed_ref, f32[128,2048]{1,0:T(8,128)} %get-tuple-element.29.local_ref, ...), custom_call_target="tpu_custom_call" | custom-call | tf_op jit(solution)/shard_map/pallas_call | solution.py:365
  166.5 2.0 %copy.29 = bf16[128,2048]{1,0:T(8,128)(2,1)} copy(bf16[128,2048]{1,0:T(8,128)(2,1)} %get-tuple-element.56) | data formatting | bytes 1048576
  168.5 1.9 %copy.30 = bf16[128,2048]{1,0:T(8,128)(2,1)} copy(bf16[128,2048]{1,0:T(8,128)(2,1)} %get-tuple-element.57) | data formatting | bytes 1048576
  170.4 0.8 copy.31
  171.2 1.1 copy.32
  (9 shorter events, 0.0 us)
Async XLA Ops:
  57.6 7.4 %copy-start = (f32[128,2048]{1,0:T(8,128)S(1)}, f32[128,2048]{1,0:T(8,128)}, u32[]{:S(2)}) copy-start(f32[128,2048]{1,0:T(8,128)} %get-tuple-element.25) | copy-start | bytes 3145732
  57.6 9.1 %copy-start.3 = (bf16[2,128,1536]{2,1,0:T(8,128)(2,1)S(1)}, bf16[2,128,1536]{2,1,0:T(8,128)(2,1)}, u32[]{:S(2)}) copy-start(bf16[2,128,1536]{2,1,0:T(8,128)(2,1)} %get-tuple-element.28) | copy-start | bytes 2359300
  59.0 6.0 %collective-permute-start.1 = (bf16[128,2048]{1,0:T(8,128)(2,1)S(1)}, bf16[128,2048]{1,0:T(8,128)(2,1)S(1)}, u32[]{:S(2)}, u32[]{:S(2)}) collective-permute-start(bf16[128,2048]{1,0:T(8,128)(2,1)S(1)} %convert_element_type.133), channel_id=1, source_target_pairs={{0,2},{1,3},{8,10},{9,11},{16,18},{17,19},{24,26},{25,27}} | collective-permute-start | bytes 1572872 | tf_op jit(solution)/shard_map/ppermute | solution.py:398
  62.2 2.1 %collective-permute-start = (f32[1,128]{1,0:T(1,128)S(1)}, f32[1,128]{1,0:T(1,128)S(1)}, u32[]{:S(2)}, u32[]{:S(2)}) collective-permute-start(f32[1,128]{1,0:T(1,128)S(1)} %broadcast_in_dim.10), channel_id=1, source_target_pairs={{0,2},{2,4},{4,6},{1,3},{3,5},{5,7},{8,10},{10,12},{12,14},{9,11},... | collective-permute-start | bytes 1544 | tf_op jit(solution)/shard_map/ppermute | solution.py:390
  65.2 11.8 %collective-permute-start.2 = (bf16[128,2048]{1,0:T(8,128)(2,1)S(1)}, bf16[128,2048]{1,0:T(8,128)(2,1)}, u32[]{:S(2)}, u32[]{:S(2)}) collective-permute-start(bf16[128,2048]{1,0:T(8,128)(2,1)S(1)} %add_convert_fusion.1), channel_id=1, source_target_pairs={{2,4},{3,5},{10,12},{11,13},{18,20},{19,21},{26,28},{27,29}} | collective-permute-start | bytes 1572872 | tf_op jit(solution)/shard_map/ppermute | solution.py:398
  67.9 28.1 %all-to-all-start = ((bf16[16,192,128]{2,1,0:T(8,128)(2,1)}), bf16[16,192,128]{2,1,0:T(8,128)(2,1)S(1)}, u32[]{:S(2)}, u32[]{:S(2)}) async-start(bf16[16,192,128]{2,1,0:T(8,128)(2,1)} %bitcast.11), calls=%async_computation | async-start | bytes 1572864 | tf_op jit(solution)/shard_map/all_to_all | solution.py:435
  77.0 6.4 %copy-start.5 = (s32[1,128]{1,0:T(1,128)S(1)}, s32[1,128]{1,0:T(1,128)}, u32[]{:S(2)}) copy-start(s32[1,128]{1,0:T(1,128)} %param.12) | copy-start | bytes 1540
  78.3 8.0 %collective-permute-start.3 = (bf16[128,2048]{1,0:T(8,128)(2,1)S(1)}, bf16[128,2048]{1,0:T(8,128)(2,1)S(1)}, u32[]{:S(2)}, u32[]{:S(2)}) collective-permute-start(bf16[128,2048]{1,0:T(8,128)(2,1)S(1)} %get-tuple-element.37), channel_id=1, source_target_pairs={{4,6},{5,7},{12,14},{13,15},{20,22},{21,23},{28,30},{29,31}} | collective-permute-start | bytes 1572872 | tf_op jit(solution)/shard_map/ppermute | solution.py:398
  79.6 3.1 %collective-permute-start.4 = (f32[1,128]{1,0:T(1,128)S(1)}, f32[1,128]{1,0:T(1,128)S(1)}, u32[]{:S(2)}, u32[]{:S(2)}) collective-permute-start(f32[1,128]{1,0:T(1,128)S(1)} %broadcast_in_dim.12), channel_id=1, source_target_pairs={{2,0},{4,2},{6,4},{3,1},{5,3},{7,5},{10,8},{12,10},{14,12},{11,9},... | collective-permute-start | bytes 1544 | tf_op jit(solution)/shard_map/ppermute | solution.py:390
  95.9 0.9 copy-start.1
  166.4 3.9 %copy-start.4 = (bf16[128,2048]{1,0:T(8,128)(2,1)S(1)}, bf16[128,2048]{1,0:T(8,128)(2,1)}, u32[]{:S(2)}) copy-start(bf16[128,2048]{1,0:T(8,128)(2,1)} %get-tuple-element.58) | copy-start | bytes 1572868
  166.5 4.7 %copy-start.2 = (f32[192,2048]{1,0:T(8,128)S(1)}, f32[192,2048]{1,0:T(8,128)}, u32[]{:S(2)}) copy-start(f32[192,2048]{1,0:T(8,128)} %get-tuple-element.59) | copy-start | bytes 4718596
